TPU v7x, 512 devices: a whole 4x8x8 slice. The times are simulated.
512 devices in a mesh: uly: 8 (over y_hi, core), blk: 64 (over z, x, y_lo).
Axes of the slice: x: 4, y: 8 (y_hi: 4, y_lo: 2; y = y_hi * 2 + y_lo), z: 8, core: 2. Of those that a mesh axis runs over, the one named last changes fastest.
Arguments:
- query_proj: bfloat16 [192, 384, 3072], P('blk', 'uly'), may hold values from -16 to 16
- key_proj: bfloat16 [192, 384, 3072], P('blk', 'uly'), may hold values from -16 to 16
- value_proj: bfloat16 [192, 384, 3072], P('blk', 'uly'), may hold values from -6 to 6
- query_gain: float32 [128], replicated, may hold values from 0.5 to 8
- key_gain: float32 [128], replicated, may hold values from 0.5 to 8
- neighbours: int32 [192, 9], P('blk'), may hold values from 0 to 191, as said below
- tile_counts: int32 [192], P('blk'), may hold values from 1 to 9, as said below
Outputs:
- attention: bfloat16 [192, 384, 3072], P('blk', 'uly')
Inputs may be any that keep to these rules, and one draw needn't show every extreme that they name: `neighbours`: the first tile_counts[t] entries of row t are distinct tiles; entry 0 is t itself; every entry lies in the slab of tile t or in one of the two slabs beside it, a slab being the tiles with equal index // 3; entries at positions tile_counts[t] and beyond equal t. `tile_counts`: some tile lists 9 tiles.
All inputs are finite; a program needn't handle non-finite values.
Results may differ from a plain program's by a relative error of at most 0.005.
The roundings to bfloat16 on the way count: a program that leaves them out, or rounds other values in their place, can miss the bound.
Values may be sent and summed in bfloat16 or wider, within the bound.
No kernel may reach another device: no remote copies, remote signals or barrier semaphores. Data moves between devices by JAX's collectives and lax.ppermute only.
A program may use at most 128 MiB of HBM per device.

v0:
```python
import functools
import math

import jax
import jax.numpy as jnp
import numpy as np
from jax import lax
from jax.experimental import pallas as pl
from jax.experimental.pallas import tpu as pltpu
from jax.sharding import Mesh
from jax.sharding import PartitionSpec as P


HD = 128
NB = 9
TD = 3
LOC = 48
COLS = 8 * 4
SIZES = (4, 2, 8, 4, 2)
AXES = ("yhi", "core", "z", "x", "ylo")
RING = ("ylo", "yhi")
CHUNKS = ((0,), (1, 2))
ROWS = 4 * LOC
KEYS = 8 * LOC
GROUP = {1: 9, 2: 3}
STEPS = {"first": 2 * TD, "last": TD, "all": 3 * TD}
EXP_SCALE = math.log2(math.e) / math.sqrt(HD)


def route(move):
    pairs = []
    for i, at in enumerate(np.ndindex(*SIZES)):
        to = move(*at)
        if to is not None:
            pairs.append((i, int(np.ravel_multi_index(to, SIZES))))
    return pairs


def to_column(distance):
    def move(u, c, z, x, p):
        n = z * 4 + x + distance
        return (u, c, n // 4, n % 4, p) if 0 <= n < COLS else None

    return route(move)


SWAP_CORE = route(lambda u, c, z, x, p: (u, 1 - c, z, x, p))
SWAP_SLAB = route(lambda u, c, z, x, p: (u, c, z, x, 1 - p))
FORWARD = to_column(1)
BACKWARD = to_column(-1)


def pack_kernel(heads, q_ref, k_ref, v_ref, qg_ref, kg_ref, out_ref):
    for which, (ref, gain) in enumerate(((q_ref, qg_ref), (k_ref, kg_ref), (v_ref, None))):
        for chip in range(8):
            for slot, head in enumerate(heads):
                at = (chip * 3 + head) * HD
                part = ref[0, :, at : at + HD]
                if gain is not None:
                    wide = part.astype(jnp.float32)
                    mean = jnp.mean(wide * wide, axis=-1, keepdims=True)
                    part = (wide * lax.rsqrt(mean + 1e-06) * gain[...]).astype(jnp.bfloat16)
                out_ref[chip, which, 0, :, slot * HD : (slot + 1) * HD] = part


def pack(heads, query, key, value, query_gain, key_gain):
    width = len(heads) * HD
    block = pl.BlockSpec((1, LOC, 24 * HD), lambda t: (t, 0, 0))
    gain = pl.BlockSpec((1, HD), lambda t: (0, 0))
    return pl.pallas_call(
        functools.partial(pack_kernel, heads),
        grid=(TD,),
        in_specs=[block] * 3 + [gain] * 2,
        out_specs=pl.BlockSpec((8, 3, 1, LOC, width), lambda t: (0, 0, t, 0, 0)),
        out_shape=jax.ShapeDtypeStruct((8, 3, TD, LOC, width), jnp.bfloat16),
    )(query, key, value, query_gain.reshape(1, HD), key_gain.reshape(1, HD))


def attend_kernel(part, nh, live_ref, *refs):
    copies = []
    refs = list(refs)
    sems = refs.pop()
    lbuf, abuf, mbuf, sbuf, vbuf, kbuf, qbuf = (refs.pop() for _ in range(7))
    own = refs.pop(0)
    carry = None
    if part == "first":
        mate = refs.pop(0)
    elif part == "last":
        prev_own, prev_mate, next_own, next_mate = (refs.pop(0) for _ in range(4))
        carry = [refs.pop(0) for _ in range(3)]
    else:
        mate, prev_own, prev_mate, next_own, next_mate = (refs.pop(0) for _ in range(5))
    outs = refs
    tiles = STEPS[part]
    group_size = min(tiles, GROUP[nh])

    def fetch(src, dst):
        copy = pltpu.make_async_copy(src, dst, sems.at[len(copies)])
        copy.start()
        copies.append(copy)

    for p in range(2):
        for u in range(4):
            rows = slice(u * LOC, (u + 1) * LOC)
            fetch(own.at[p * 4 + u, 0], qbuf.at[p * TD : (p + 1) * TD, rows])
    for half in range(2):
        for u in range(4):
            rows = slice((half * 4 + u) * LOC, (half * 4 + u + 1) * LOC)
            for kv, buf in enumerate((kbuf, vbuf)):
                parts = []
                if part != "first":
                    parts.append((prev_own, prev_mate)[half].at[u, kv])
                if part != "last":
                    column = (own, mate)[half]
                    parts += [column.at[u, 1 + kv], column.at[4 + u, 1 + kv]]
                if part != "first":
                    parts.append((next_own, next_mate)[half].at[u, kv])
                for slab, src in enumerate(parts):
                    fetch(src, buf.at[slab * TD : (slab + 1) * TD, rows])
    for copy in copies:
        copy.wait()

    def lanes(h):
        return slice(h * HD, (h + 1) * HD)

    def key_tile(tile, j):
        return j if part == "first" else tile // TD * TD + j

    def is_live(tile, j):
        slab = tile // TD
        at = {"first": j + TD * (1 - slab), "last": j + 2 * TD * slab, "all": j}[part]
        return live_ref[tile, at] > 0

    def step(group, tile, ahead):
        for i in range(group_size):
            j = group * group_size + i
            if tile is not None:
                listed = key_tile(tile, j)
                live = is_live(tile, j)
                slot = tile % 2
                for h in range(nh):
                    top = jnp.where(live, mbuf[slot, h], 1e30)
                    parts = [
                        jnp.exp2((sbuf[slot, h, j, :, lanes(g)] - top) * EXP_SCALE)
                        for g in range(KEYS // 128)
                    ]
                    lbuf[h] += sum(parts[1:], parts[0])
                    rounded = jnp.concatenate([p.astype(jnp.bfloat16) for p in parts], axis=-1)
                    abuf[h] += jnp.dot(
                        rounded, vbuf[listed, :, lanes(h)], preferred_element_type=jnp.float32
                    )
            if ahead is not None:
                listed = key_tile(ahead, j)
                live = is_live(ahead, j)
                slot = ahead % 2
                for h in range(nh):
                    scores = lax.dot_general(
                        qbuf[ahead, :, lanes(h)], kbuf[listed, :, lanes(h)],
                        (((1,), (1,)), ((), ())), preferred_element_type=jnp.float32,
                    )
                    sbuf[slot, h, j] = scores
                    top = functools.reduce(
                        jnp.maximum, [scores[:, lanes(g)] for g in range(KEYS // 128)]
                    )
                    mbuf[slot, h] = jnp.maximum(mbuf[slot, h], jnp.where(live, top, -1e30))

    def sweep(tile, ahead):
        if tile is not None:
            for h in range(nh):
                if carry is None:
                    lbuf[h] = jnp.zeros(lbuf.shape[1:], jnp.float32)
                    abuf[h] = jnp.zeros(abuf.shape[1:], jnp.float32)
                else:
                    top, total, sums = (ref[tile, h] for ref in carry)
                    scale = jnp.exp2((top - mbuf[tile % 2, h]) * EXP_SCALE)
                    lbuf[h] = total * scale
                    abuf[h] = sums * scale
        if ahead is not None:
            if carry is None:
                mbuf[ahead % 2] = jnp.full(mbuf.shape[1:], -1e30, jnp.float32)
            else:
                mbuf[ahead % 2] = carry[0][ahead]

        @pl.loop(0, tiles // group_size)
        def _(group):
            step(group, tile, ahead)

        for h in range(nh):
            if ahead is not None:
                top = jnp.max(mbuf[ahead % 2, h], axis=-1, keepdims=True)
                mbuf[ahead % 2, h] = jnp.broadcast_to(top, (ROWS, 128))
            if tile is not None and part == "first":
                outs[0][tile, h] = mbuf[tile % 2, h]
                outs[1][tile, h] = lbuf[h]
                outs[2][tile, h] = abuf[h]
            elif tile is not None:
                total = jnp.sum(lbuf[h], axis=-1, keepdims=True)
                result = (abuf[h] / total).astype(jnp.bfloat16)
                for u in range(4):
                    at = tile // TD * 4 + u
                    outs[0][at, tile % TD, :, lanes(h)] = result[u * LOC : (u + 1) * LOC]

    sweep(None, 0)

    @pl.loop(0, 2 * TD - 1)
    def _(tile):
        sweep(tile, tile + 1)

    sweep(2 * TD - 1, None)


def attend(part, live, arrays, carry=()):
    width = arrays[0].shape[-1]
    nh = width // HD
    whole = pl.BlockSpec(memory_space=pltpu.VMEM)
    if part == "first":
        shapes = [jax.ShapeDtypeStruct((2 * TD, nh, ROWS, 128), jnp.float32)] * 3
    else:
        shapes = [jax.ShapeDtypeStruct((8, TD, LOC, width), jnp.bfloat16)]
    held = {"first": 2, "last": 2, "all": 4}[part] * TD
    return pl.pallas_call(
        functools.partial(attend_kernel, part, nh),
        in_specs=[pl.BlockSpec(memory_space=pltpu.SMEM)]
        + [pl.BlockSpec(memory_space=pl.ANY)] * len(arrays)
        + [whole] * len(carry),
        out_specs=[whole] * len(shapes),
        out_shape=shapes,
        scratch_shapes=[
            pltpu.VMEM((2 * TD, ROWS, width), jnp.bfloat16),
            pltpu.VMEM((held, KEYS, width), jnp.bfloat16),
            pltpu.VMEM((held, KEYS, width), jnp.bfloat16),
            pltpu.VMEM((2, nh, STEPS[part], ROWS, KEYS), jnp.float32),
            pltpu.VMEM((2, nh, ROWS, 128), jnp.float32),
            pltpu.VMEM((nh, ROWS, HD), jnp.float32),
            pltpu.VMEM((nh, ROWS, 128), jnp.float32),
            pltpu.SemaphoreType.DMA((72,)),
        ],
        compiler_params=pltpu.CompilerParams(vmem_limit_bytes=24 << 20),
    )(live, *arrays, *carry)


def unpack_kernel(*refs):
    out_ref = refs[-1]
    for ref, heads in zip(refs, CHUNKS):
        width = len(heads) * HD
        for chip in range(8):
            at = (chip * 3 + heads[0]) * HD
            out_ref[0, :, at : at + width] = ref[chip, 0]


def unpack(*blocks):
    return pl.pallas_call(
        unpack_kernel,
        grid=(TD,),
        in_specs=[
            pl.BlockSpec((8, 1, LOC, b.shape[-1]), lambda t: (0, t, 0, 0)) for b in blocks
        ],
        out_specs=pl.BlockSpec((1, LOC, 24 * HD), lambda t: (t, 0, 0)),
        out_shape=jax.ShapeDtypeStruct((TD, LOC, 24 * HD), jnp.bfloat16),
        name="unpack",
    )(*blocks)


def compute(query_proj, key_proj, value_proj, query_gain, key_gain, neighbours, tile_counts):
    slab = lax.axis_index("ylo")
    column = lax.axis_index("z") * SIZES[3] + lax.axis_index("x")
    table = jnp.concatenate([neighbours, tile_counts[:, None]], axis=1)
    other = lax.ppermute(table, AXES, SWAP_SLAB)
    table = jnp.where(slab == 0, jnp.stack([table, other]), jnp.stack([other, table]))
    table = table.reshape(2 * TD, NB + 1)
    first_tile = (2 * column - 1) * TD + TD * (jnp.arange(2 * TD, dtype=jnp.int32) // TD)
    local = table[:, :NB] - first_tile[:, None]
    place = jnp.arange(NB, dtype=jnp.int32)
    counted = place[None, :] < table[:, NB:]
    match = (local[:, None, :] == place[None, :, None]) & counted[:, None, :]
    live = jnp.any(match, axis=2).astype(jnp.int32)

    returned = []
    for i, heads in enumerate(CHUNKS):
        block = pack(heads, query_proj, key_proj, value_proj, query_gain, key_gain)
        own = lax.all_to_all(block, RING, 0, 0, tiled=True)
        prev_own = lax.ppermute(own[4:, 1:], AXES, FORWARD)
        next_own = lax.ppermute(own[:4, 1:], AXES, BACKWARD)
        mate = lax.ppermute(own, AXES, SWAP_CORE)
        prev_mate = lax.ppermute(prev_own, AXES, SWAP_CORE)
        next_mate = lax.ppermute(next_own, AXES, SWAP_CORE)
        halo = [prev_own, prev_mate, next_own, next_mate]
        if i == len(CHUNKS) - 1:
            carry = attend("first", live, [own, mate])
            (done,) = attend("last", live, [own, *halo], carry)
        else:
            (done,) = attend("all", live, [own, mate, *halo])
        returned.append(lax.all_to_all(done, RING, 0, 0, tiled=True))
    return unpack(*returned)


def solution(mesh):
    split = Mesh(mesh.devices.reshape(SIZES), AXES)
    blk, uly = ("z", "x", "ylo"), ("yhi", "core")
    rows = P(blk, uly, None)
    in_specs = (rows, rows, rows, P(), P(), P(blk, None), P(blk))
    return jax.shard_map(compute, mesh=split, in_specs=in_specs, out_specs=rows, check_vma=False)
```

profile of v0, /device:TPU:198, one launch (start us, length us, event | category | flops | bytes accessed | tf_op | source)
XLA Modules:
  0.0 198.2 jit_solution(7704598552924292259)
XLA Ops:
  0.0 4.2 %shard_map.75 = bf16[8,3,3,48,256]{4,3,2,1,0:T(8,128)(2,1)} custom-call(bf16[3,48,3072]{2,1,0:T(8,128)(2,1)} %q_ref.3, bf16[3,48,3072]{2,1,0:T(8,128)(2,1)} %k_ref.3, bf16[3,48,3072]{2,1,0:T(8,128)(2,1)} %v_ref.3, f32[1,128]{1,0:T(1,128)} %bitcast.6, f32[1,128]{1,0:T(1,128)} %bitcast.8), custom_call_target="tpu_custom_call" | custom-call | tf_op jit(solution)/shard_map/pallas_call | solution.py:70
  4.2 7.1 %all-to-all-start.2 = ((bf16[8,3,3,48,256]{4,3,2,1,0:T(8,128)(2,1)}), bf16[8,3,3,48,256]{4,3,2,1,0:T(8,128)(2,1)S(1)}, u32[]{:S(2)}, u32[]{:S(2)}) async-start(bf16[8,3,3,48,256]{4,3,2,1,0:T(8,128)(2,1)} %shard_map.75), calls=%async_computation.2 | async-start | bytes 3538944 | tf_op jit(solution)/shard_map/all_to_all | solution.py:281
  11.3 3.7 %shard_map.73 = bf16[8,3,3,48,128]{4,3,2,1,0:T(8,128)(2,1)} custom-call(bf16[3,48,3072]{2,1,0:T(8,128)(2,1)} %q_ref.3, bf16[3,48,3072]{2,1,0:T(8,128)(2,1)} %k_ref.3, bf16[3,48,3072]{2,1,0:T(8,128)(2,1)} %v_ref.3, f32[1,128]{1,0:T(1,128)} %bitcast.7, f32[1,128]{1,0:T(1,128)} %bitcast.9), custom_call_target="tpu_custom_call" | custom-call | tf_op jit(solution)/shard_map/pallas_call | solution.py:70
  14.9 37.8 %all-to-all-done.2.refs_0_ = bf16[8,3,3,48,256]{4,3,2,1,0:T(8,128)(2,1)S(1)} async-done(((bf16[8,3,3,48,256]{4,3,2,1,0:T(8,128)(2,1)}), bf16[8,3,3,48,256]{4,3,2,1,0:T(8,128)(2,1)S(1)}, u32[]{:S(2)}, u32[]{:S(2)}) %all-to-all-start.2) | async-done | bytes 1769504 | tf_op jit(solution)/shard_map/all_to_all | solution.py:281
  52.7 4.7 %all-to-all-start = ((bf16[8,3,3,48,128]{4,3,2,1,0:T(8,128)(2,1)}), bf16[8,3,3,48,128]{4,3,2,1,0:T(8,128)(2,1)S(1)}, u32[]{:S(2)}, u32[]{:S(2)}) async-start(bf16[8,3,3,48,128]{4,3,2,1,0:T(8,128)(2,1)} %shard_map.73), calls=%async_computation | async-start | bytes 1769472 | tf_op jit(solution)/shard_map/all_to_all | solution.py:281
  57.6 3.9 %collective-permute-start = (s32[3,10]{1,0:T(4,128)S(1)}, s32[3,10]{1,0:T(4,128)S(1)}, u32[]{:S(2)}, u32[]{:S(2)}) collective-permute-start(s32[3,10]{1,0:T(4,128)S(1)} %pad_add_fusion), channel_id=1, source_target_pairs={{0,1},{1,0},{2,3},{3,2},{4,5},{5,4},{6,7},{7,6},{8,9},{9,8},{10,11... | collective-permute-start | bytes 368 | tf_op jit(solution)/shard_map/ppermute | solution.py:268
  61.6 1.9 collective-permute-start.10
  63.5 16.2 %all-to-all-done.refs_0_ = bf16[8,3,3,48,128]{4,3,2,1,0:T(8,128)(2,1)S(1)} async-done(((bf16[8,3,3,48,128]{4,3,2,1,0:T(8,128)(2,1)}), bf16[8,3,3,48,128]{4,3,2,1,0:T(8,128)(2,1)S(1)}, u32[]{:S(2)}, u32[]{:S(2)}) %all-to-all-start) | async-done | bytes 884768 | tf_op jit(solution)/shard_map/all_to_all | solution.py:281
  80.6 5.4 %collective-permute-start.2 = (bf16[4,2,3,48,128]{4,3,2,1,0:T(8,128)(2,1)}, bf16[4,2,3,48,128]{4,3,2,1,0:T(8,128)(2,1)}, u32[]{:S(2)}, u32[]{:S(2)}) collective-permute-start(bf16[4,2,3,48,128]{4,3,2,1,0:T(8,128)(2,1)} %get-tuple-element.14), channel_id=1, source_target_pairs={{0,2},{1,3},{2,4},{3,5},{4,6},{5,7},{6,8},{7,9},{8,10},{9,11},{10,... | collective-permute-start | bytes 884744 | tf_op jit(solution)/shard_map/ppermute | solution.py:282
  86.0 1.9 collective-permute-start.4
  88.0 1.9 collective-permute-start.1
  91.0 7.2 %collective-permute-start.6 = (bf16[4,2,3,48,256]{4,3,2,1,0:T(8,128)(2,1)}, bf16[4,2,3,48,256]{4,3,2,1,0:T(8,128)(2,1)}, u32[]{:S(2)}, u32[]{:S(2)}) collective-permute-start(bf16[4,2,3,48,256]{4,3,2,1,0:T(8,128)(2,1)} %get-tuple-element.12), channel_id=1, source_target_pairs={{0,2},{1,3},{2,4},{3,5},{4,6},{5,7},{6,8},{7,9},{8,10},{9,11},{10,... | collective-permute-start | bytes 1769480 | tf_op jit(solution)/shard_map/ppermute | solution.py:282
  98.3 1.9 collective-permute-start.8
  100.3 2.1 %collective-permute-start.3 = (bf16[4,2,3,48,128]{4,3,2,1,0:T(8,128)(2,1)}, bf16[4,2,3,48,128]{4,3,2,1,0:T(8,128)(2,1)S(1)}, u32[]{:S(2)}, u32[]{:S(2)}) collective-permute-start(bf16[4,2,3,48,128]{4,3,2,1,0:T(8,128)(2,1)} %collective-permute-done.2.refs_2_), channel_id=1, source_target_pairs={{0,64},{1,65},{2,66},{3,67},{4,68},{5,69},{6,70},{7,71},{8,72},{9,... | collective-permute-start | bytes 884744 | tf_op jit(solution)/shard_map/ppermute | solution.py:285
  104.7 2.1 %collective-permute-start.5 = (bf16[4,2,3,48,128]{4,3,2,1,0:T(8,128)(2,1)}, bf16[4,2,3,48,128]{4,3,2,1,0:T(8,128)(2,1)}, u32[]{:S(2)}, u32[]{:S(2)}) collective-permute-start(bf16[4,2,3,48,128]{4,3,2,1,0:T(8,128)(2,1)} %collective-permute-done.4.refs_4_), channel_id=1, source_target_pairs={{0,64},{1,65},{2,66},{3,67},{4,68},{5,69},{6,70},{7,71},{8,72},{9,... | collective-permute-start | bytes 884744 | tf_op jit(solution)/shard_map/ppermute | solution.py:286
  106.9 5.0 %collective-permute-done.6.refs_1_ = bf16[4,2,3,48,256]{4,3,2,1,0:T(8,128)(2,1)} collective-permute-done((bf16[4,2,3,48,256]{4,3,2,1,0:T(8,128)(2,1)}, bf16[4,2,3,48,256]{4,3,2,1,0:T(8,128)(2,1)}, u32[]{:S(2)}, u32[]{:S(2)}) %collective-permute-start.6) | collective-permute-done | bytes 589856 | tf_op jit(solution)/shard_map/ppermute | solution.py:282
  113.7 5.5 %collective-permute-done.8.refs_3_ = bf16[4,2,3,48,256]{4,3,2,1,0:T(8,128)(2,1)} collective-permute-done((bf16[4,2,3,48,256]{4,3,2,1,0:T(8,128)(2,1)}, bf16[4,2,3,48,256]{4,3,2,1,0:T(8,128)(2,1)}, u32[]{:S(2)}, u32[]{:S(2)}) %collective-permute-start.8) | collective-permute-done | bytes 589856 | tf_op jit(solution)/shard_map/ppermute | solution.py:283
  119.3 1.9 collective-permute-start.9
  122.5 15.2 %shard_map.74 = bf16[8,3,48,128]{3,2,1,0:T(8,128)(2,1)} custom-call(s32[6,9]{1,0:T(8,128)S(1)} %convert_element_type.3.live_ref, bf16[8,3,3,48,128]{4,3,2,1,0:T(8,128)(2,1)S(1)} %all-to-all-done.refs_0_, bf16[8,3,3,48,128]{4,3,2,1,0:T(8,128)(2,1)S(1)} %collective-permute-done.1.refs_1_, bf16[4,2,3,48,128]{4,3,2,1,0:T(8,128)(2,1)} %collective-permute-done.2.refs_2_, ...), custom_call_target="tpu_custom_call" | custom-call | tf_op jit(solution)/shard_map/pallas_call | solution.py:221
  137.8 4.6 %all-to-all-start.1 = ((bf16[8,3,48,128]{3,2,1,0:T(8,128)(2,1)}), bf16[8,3,48,128]{3,2,1,0:T(8,128)(2,1)S(1)}, u32[]{:S(2)}, u32[]{:S(2)}) async-start(bf16[8,3,48,128]{3,2,1,0:T(8,128)(2,1)} %shard_map.74), calls=%async_computation.1 | async-start | bytes 589824 | tf_op jit(solution)/shard_map/all_to_all | solution.py:293
  142.4 16.7 %shard_map.76 = (f32[6,2,192,128]{3,2,1,0:T(8,128)S(1)}, f32[6,2,192,128]{3,2,1,0:T(8,128)S(1)}, f32[6,2,192,128]{3,2,1,0:T(8,128)S(1)}) custom-call(s32[6,9]{1,0:T(8,128)S(1)} %convert_element_type.3.live_ref, bf16[8,3,3,48,256]{4,3,2,1,0:T(8,128)(2,1)S(1)} %all-to-all-done.2.refs_0_, bf16[8,3,3,48,256]{4,3,2,1,0:T(8,128)(2,1)} %collective-permute-done.10.refs_1_), custom_call_target="tpu_custom_call" | custom-call | tf_op jit(solution)/shard_map/pallas_call | solution.py:221
  159.1 10.3 %shard_map.77 = bf16[8,3,48,256]{3,2,1,0:T(8,128)(2,1)S(1)} custom-call(s32[6,9]{1,0:T(8,128)S(1)} %convert_element_type.3.live_ref, bf16[8,3,3,48,256]{4,3,2,1,0:T(8,128)(2,1)S(1)} %all-to-all-done.2.refs_0_, bf16[4,2,3,48,256]{4,3,2,1,0:T(8,128)(2,1)} %collective-permute-done.6.refs_1_, bf16[4,2,3,48,256]{4,3,2,1,0:T(8,128)(2,1)} %collective-permute-done.7.refs_2_, ...), custom_call_target="tpu_custom_call" | custom-call | tf_op jit(solution)/shard_map/pallas_call | solution.py:221
  169.4 25.8 %all_to_all.20.refs_1_ = bf16[8,3,48,256]{3,2,1,0:T(8,128)(2,1)} all-to-all(bf16[8,3,48,256]{3,2,1,0:T(8,128)(2,1)S(1)} %shard_map.77), channel_id=1, replica_groups=mesh['yhi'=4,'core'=2,'z'=8,'x'=4,'ylo'=2] {'ylo','yhi'}, dimensions={0} | all-to-all | bytes 1179648 | tf_op jit(solution)/shard_map/all_to_all | solution.py:293
  195.2 3.0 %unpack.1 = bf16[3,48,3072]{2,1,0:T(8,128)(2,1)} custom-call(bf16[8,3,48,128]{3,2,1,0:T(8,128)(2,1)} %copy-done.2, bf16[8,3,48,256]{3,2,1,0:T(8,128)(2,1)} %all_to_all.20.refs_1_), custom_call_target="tpu_custom_call" | custom-call | tf_op jit(solution)/shard_map/unpack/pallas_call | solution.py:252
  (35 shorter events, 7.9 us)
Async XLA Ops:
  4.2 48.6 %all-to-all-start.2 = ((bf16[8,3,3,48,256]{4,3,2,1,0:T(8,128)(2,1)}), bf16[8,3,3,48,256]{4,3,2,1,0:T(8,128)(2,1)S(1)}, u32[]{:S(2)}, u32[]{:S(2)}) async-start(bf16[8,3,3,48,256]{4,3,2,1,0:T(8,128)(2,1)} %shard_map.75), calls=%async_computation.2 | async-start | bytes 3538944 | tf_op jit(solution)/shard_map/all_to_all | solution.py:281
  14.9 42.5 %copy-start.4 = (s32[3]{0:T(128)S(1)}, s32[3]{0:T(128)}, u32[]{:S(2)}) copy-start(s32[3]{0:T(128)} %param.13) | copy-start | bytes 40
  14.9 42.6 %copy-start.3 = (s32[3,9]{1,0:T(4,128)S(1)}, s32[3,9]{1,0:T(4,128)}, u32[]{:S(2)}) copy-start(s32[3,9]{1,0:T(4,128)} %param.12) | copy-start | bytes 328
  52.7 27.0 %all-to-all-start = ((bf16[8,3,3,48,128]{4,3,2,1,0:T(8,128)(2,1)}), bf16[8,3,3,48,128]{4,3,2,1,0:T(8,128)(2,1)S(1)}, u32[]{:S(2)}, u32[]{:S(2)}) async-start(bf16[8,3,3,48,128]{4,3,2,1,0:T(8,128)(2,1)} %shard_map.73), calls=%async_computation | async-start | bytes 1769472 | tf_op jit(solution)/shard_map/all_to_all | solution.py:281
  57.6 33.5 %collective-permute-start = (s32[3,10]{1,0:T(4,128)S(1)}, s32[3,10]{1,0:T(4,128)S(1)}, u32[]{:S(2)}, u32[]{:S(2)}) collective-permute-start(s32[3,10]{1,0:T(4,128)S(1)} %pad_add_fusion), channel_id=1, source_target_pairs={{0,1},{1,0},{2,3},{3,2},{4,5},{5,4},{6,7},{7,6},{8,9},{9,8},{10,11... | collective-permute-start | bytes 368 | tf_op jit(solution)/shard_map/ppermute | solution.py:268
  61.6 80.8 %collective-permute-start.10 = (bf16[8,3,3,48,256]{4,3,2,1,0:T(8,128)(2,1)S(1)}, bf16[8,3,3,48,256]{4,3,2,1,0:T(8,128)(2,1)}, u32[]{:S(2)}, u32[]{:S(2)}) collective-permute-start(bf16[8,3,3,48,256]{4,3,2,1,0:T(8,128)(2,1)S(1)} %all-to-all-done.2.refs_0_), channel_id=1, source_target_pairs={{0,64},{1,65},{2,66},{3,67},{4,68},{5,69},{6,70},{7,71},{8,72},{9,... | collective-permute-start | bytes 5308424 | tf_op jit(solution)/shard_map/ppermute | solution.py:284
  80.6 17.7 %collective-permute-start.2 = (bf16[4,2,3,48,128]{4,3,2,1,0:T(8,128)(2,1)}, bf16[4,2,3,48,128]{4,3,2,1,0:T(8,128)(2,1)}, u32[]{:S(2)}, u32[]{:S(2)}) collective-permute-start(bf16[4,2,3,48,128]{4,3,2,1,0:T(8,128)(2,1)} %get-tuple-element.14), channel_id=1, source_target_pairs={{0,2},{1,3},{2,4},{3,5},{4,6},{5,7},{6,8},{7,9},{8,10},{9,11},{10,... | collective-permute-start | bytes 884744 | tf_op jit(solution)/shard_map/ppermute | solution.py:282
  86.0 14.2 %collective-permute-start.4 = (bf16[4,2,3,48,128]{4,3,2,1,0:T(8,128)(2,1)}, bf16[4,2,3,48,128]{4,3,2,1,0:T(8,128)(2,1)}, u32[]{:S(2)}, u32[]{:S(2)}) collective-permute-start(bf16[4,2,3,48,128]{4,3,2,1,0:T(8,128)(2,1)} %get-tuple-element.13), channel_id=1, source_target_pairs={{2,0},{3,1},{4,2},{5,3},{6,4},{7,5},{8,6},{9,7},{10,8},{11,9},{12,... | collective-permute-start | bytes 884744 | tf_op jit(solution)/shard_map/ppermute | solution.py:283
  88.0 33.6 %collective-permute-start.1 = (bf16[8,3,3,48,128]{4,3,2,1,0:T(8,128)(2,1)S(1)}, bf16[8,3,3,48,128]{4,3,2,1,0:T(8,128)(2,1)S(1)}, u32[]{:S(2)}, u32[]{:S(2)}) collective-permute-start(bf16[8,3,3,48,128]{4,3,2,1,0:T(8,128)(2,1)S(1)} %all-to-all-done.refs_0_), channel_id=1, source_target_pairs={{0,64},{1,65},{2,66},{3,67},{4,68},{5,69},{6,70},{7,71},{8,72},{9,... | collective-permute-start | bytes 2654216 | tf_op jit(solution)/shard_map/ppermute | solution.py:284
  91.0 20.8 %collective-permute-start.6 = (bf16[4,2,3,48,256]{4,3,2,1,0:T(8,128)(2,1)}, bf16[4,2,3,48,256]{4,3,2,1,0:T(8,128)(2,1)}, u32[]{:S(2)}, u32[]{:S(2)}) collective-permute-start(bf16[4,2,3,48,256]{4,3,2,1,0:T(8,128)(2,1)} %get-tuple-element.12), channel_id=1, source_target_pairs={{0,2},{1,3},{2,4},{3,5},{4,6},{5,7},{6,8},{7,9},{8,10},{9,11},{10,... | collective-permute-start | bytes 1769480 | tf_op jit(solution)/shard_map/ppermute | solution.py:282
  98.3 21.0 %collective-permute-start.8 = (bf16[4,2,3,48,256]{4,3,2,1,0:T(8,128)(2,1)}, bf16[4,2,3,48,256]{4,3,2,1,0:T(8,128)(2,1)}, u32[]{:S(2)}, u32[]{:S(2)}) collective-permute-start(bf16[4,2,3,48,256]{4,3,2,1,0:T(8,128)(2,1)} %get-tuple-element.11), channel_id=1, source_target_pairs={{2,0},{3,1},{4,2},{5,3},{6,4},{7,5},{8,6},{9,7},{10,8},{11,9},{12,... | collective-permute-start | bytes 1769480 | tf_op jit(solution)/shard_map/ppermute | solution.py:283
  100.3 3.7 %collective-permute-start.3 = (bf16[4,2,3,48,128]{4,3,2,1,0:T(8,128)(2,1)}, bf16[4,2,3,48,128]{4,3,2,1,0:T(8,128)(2,1)S(1)}, u32[]{:S(2)}, u32[]{:S(2)}) collective-permute-start(bf16[4,2,3,48,128]{4,3,2,1,0:T(8,128)(2,1)} %collective-permute-done.2.refs_2_), channel_id=1, source_target_pairs={{0,64},{1,65},{2,66},{3,67},{4,68},{5,69},{6,70},{7,71},{8,72},{9,... | collective-permute-start | bytes 884744 | tf_op jit(solution)/shard_map/ppermute | solution.py:285
  104.0 0.7 copy-start
  104.7 16.9 %collective-permute-start.5 = (bf16[4,2,3,48,128]{4,3,2,1,0:T(8,128)(2,1)}, bf16[4,2,3,48,128]{4,3,2,1,0:T(8,128)(2,1)}, u32[]{:S(2)}, u32[]{:S(2)}) collective-permute-start(bf16[4,2,3,48,128]{4,3,2,1,0:T(8,128)(2,1)} %collective-permute-done.4.refs_4_), channel_id=1, source_target_pairs={{0,64},{1,65},{2,66},{3,67},{4,68},{5,69},{6,70},{7,71},{8,72},{9,... | collective-permute-start | bytes 884744 | tf_op jit(solution)/shard_map/ppermute | solution.py:286
  111.8 47.2 %collective-permute-start.7 = (bf16[4,2,3,48,256]{4,3,2,1,0:T(8,128)(2,1)}, bf16[4,2,3,48,256]{4,3,2,1,0:T(8,128)(2,1)}, u32[]{:S(2)}, u32[]{:S(2)}) collective-permute-start(bf16[4,2,3,48,256]{4,3,2,1,0:T(8,128)(2,1)} %collective-permute-done.6.refs_1_), channel_id=1, source_target_pairs={{0,64},{1,65},{2,66},{3,67},{4,68},{5,69},{6,70},{7,71},{8,72},{9,... | collective-permute-start | bytes 1769480 | tf_op jit(solution)/shard_map/ppermute | solution.py:285
  119.3 39.8 %collective-permute-start.9 = (bf16[4,2,3,48,256]{4,3,2,1,0:T(8,128)(2,1)}, bf16[4,2,3,48,256]{4,3,2,1,0:T(8,128)(2,1)}, u32[]{:S(2)}, u32[]{:S(2)}) collective-permute-start(bf16[4,2,3,48,256]{4,3,2,1,0:T(8,128)(2,1)} %collective-permute-done.8.refs_3_), channel_id=1, source_target_pairs={{0,64},{1,65},{2,66},{3,67},{4,68},{5,69},{6,70},{7,71},{8,72},{9,... | collective-permute-start | bytes 1769480 | tf_op jit(solution)/shard_map/ppermute | solution.py:286
  121.6 1.0 copy-start.1
  137.8 31.6 %all-to-all-start.1 = ((bf16[8,3,48,128]{3,2,1,0:T(8,128)(2,1)}), bf16[8,3,48,128]{3,2,1,0:T(8,128)(2,1)S(1)}, u32[]{:S(2)}, u32[]{:S(2)}) async-start(bf16[8,3,48,128]{3,2,1,0:T(8,128)(2,1)} %shard_map.74), calls=%async_computation.1 | async-start | bytes 589824 | tf_op jit(solution)/shard_map/all_to_all | solution.py:293
  169.4 25.8 %copy-start.2 = (bf16[8,3,48,128]{3,2,1,0:T(8,128)(2,1)}, bf16[8,3,48,128]{3,2,1,0:T(8,128)(2,1)S(1)}, u32[]{:S(2)}) copy-start(bf16[8,3,48,128]{3,2,1,0:T(8,128)(2,1)S(1)} %all-to-all-done.1.refs_0_) | copy-start | bytes 884740
where the time goes:
time: 199 us; the launch traced here: 198 us
  waiting for transfers between devices  65.9 us (33%)
  Pallas kernels  53 us (27%)
  starting transfers between devices  48.6 us (24%)
  blocking collectives  25.8 us (13%)
  local copies, waits for them, and re-layouts  4.08 us (2%)
    all_to_all x2, waiting for transfers between devices, compute(): own = lax.all_to_all(block, RING, 0, 0, tiled=True)  54.1 us
    pallas_call x3, Pallas kernels, attend(): pl.pallas_call(functools.partial(attend_kernel, part, nh), in_specs=[pl.B...  42.2 us
    all_to_all x1, blocking collectives, compute(): returned.append(lax.all_to_all(done, RING, 0, 0, tiled=True))  25.8 us
    ppermute x2, starting transfers between devices, compute(): prev_own = lax.ppermute(own[4:, 1:], AXES, FORWARD)  12.6 us
    all_to_all x2, starting transfers between devices, compute(): own = lax.all_to_all(block, RING, 0, 0, tiled=True)  11.8 us
    pallas_call x2, Pallas kernels, pack(): pl.pallas_call(functools.partial(pack_kernel, heads), grid=(TD,), in_spec...  7.82 us
    ppermute x2, waiting for transfers between devices, compute(): next_own = lax.ppermute(own[:4, 1:], AXES, BACKWARD)  5.53 us
    ppermute x2, waiting for transfers between devices, compute(): prev_own = lax.ppermute(own[4:, 1:], AXES, FORWARD)  4.97 us
  transfers between devices with their start and end apart: 14, of which 5 were waited for; matrix products, arithmetic and copies ran while one was open for 2% of the time, Pallas kernels for 23%

commit v1 on v0

v1 whole, which is shorter than its diff:
```python
import functools
import math

import jax
import jax.numpy as jnp
import numpy as np
from jax import lax
from jax.experimental import pallas as pl
from jax.experimental.pallas import tpu as pltpu
from jax.sharding import Mesh
from jax.sharding import PartitionSpec as P


HD = 128
NB = 9
TD = 3
LOC = 48
COLS = 8 * 4
SIZES = (4, 2, 8, 4, 2)
AXES = ("yhi", "core", "z", "x", "ylo")
RING = ("ylo", "yhi")
CHUNKS = ((0,), (1, 2))
ROWS = 4 * LOC
KEYS = 8 * LOC
SLABS = {"first": 2, "last": 1, "all": 3}
EXP_SCALE = math.log2(math.e) / math.sqrt(HD)


def route(move):
    pairs = []
    for i, at in enumerate(np.ndindex(*SIZES)):
        to = move(*at)
        if to is not None:
            pairs.append((i, int(np.ravel_multi_index(to, SIZES))))
    return pairs


def to_column(distance):
    def move(u, c, z, x, p):
        n = z * 4 + x + distance
        return (u, c, n // 4, n % 4, p) if 0 <= n < COLS else None

    return route(move)


SWAP_CORE = route(lambda u, c, z, x, p: (u, 1 - c, z, x, p))
SWAP_SLAB = route(lambda u, c, z, x, p: (u, c, z, x, 1 - p))
FORWARD = to_column(1)
BACKWARD = to_column(-1)


def pack_kernel(heads, q_ref, k_ref, v_ref, qg_ref, kg_ref, out_ref):
    for which, (ref, gain) in enumerate(((q_ref, qg_ref), (k_ref, kg_ref), (v_ref, None))):
        for chip in range(8):
            for slot, head in enumerate(heads):
                at = (chip * 3 + head) * HD
                part = ref[:, :, at : at + HD]
                if gain is not None:
                    wide = part.astype(jnp.float32)
                    mean = jnp.mean(wide * wide, axis=-1, keepdims=True)
                    part = (wide * lax.rsqrt(mean + 1e-06) * gain[...]).astype(jnp.bfloat16)
                out_ref[chip, which, :, :, slot * HD : (slot + 1) * HD] = part


def pack(heads, query, key, value, query_gain, key_gain):
    width = len(heads) * HD
    whole = pl.BlockSpec(memory_space=pltpu.VMEM)
    return pl.pallas_call(
        functools.partial(pack_kernel, heads),
        in_specs=[whole] * 5,
        out_specs=whole,
        out_shape=jax.ShapeDtypeStruct((8, 3, TD, LOC, width), jnp.bfloat16),
    )(query, key, value, query_gain.reshape(1, HD), key_gain.reshape(1, HD))


def attend_kernel(part, nh, live_ref, *refs):
    copies = []
    refs = list(refs)
    sems = refs.pop()
    lbuf, abuf, mbuf, sbuf, vbuf, kbuf, qbuf = (refs.pop() for _ in range(7))
    own = refs.pop(0)
    carry = None
    if part == "first":
        mate = refs.pop(0)
    elif part == "last":
        prev_own, prev_mate, next_own, next_mate = (refs.pop(0) for _ in range(4))
        carry = [refs.pop(0) for _ in range(3)]
    else:
        mate, prev_own, prev_mate, next_own, next_mate = (refs.pop(0) for _ in range(5))
    early = refs.pop(0) if len(refs) == 2 else None
    outs = refs
    base = 0 if early is None else early.shape[-1]
    groups = SLABS[part]

    def fetch(src, dst):
        copy = pltpu.make_async_copy(src, dst, sems.at[len(copies)])
        copy.start()
        copies.append(copy)

    for p in range(2):
        for u in range(4):
            rows = slice(u * LOC, (u + 1) * LOC)
            fetch(own.at[p * 4 + u, 0], qbuf.at[p * TD : (p + 1) * TD, rows])
    for half in range(2):
        for u in range(4):
            rows = slice((half * 4 + u) * LOC, (half * 4 + u + 1) * LOC)
            for kv, buf in enumerate((kbuf, vbuf)):
                parts = []
                if part != "first":
                    parts.append((prev_own, prev_mate)[half].at[u, kv])
                if part != "last":
                    column = (own, mate)[half]
                    parts += [column.at[u, 1 + kv], column.at[4 + u, 1 + kv]]
                if part != "first":
                    parts.append((next_own, next_mate)[half].at[u, kv])
                for slab, src in enumerate(parts):
                    fetch(src, buf.at[slab * TD : (slab + 1) * TD, rows])
    for copy in copies:
        copy.wait()

    def lanes(h):
        return slice(h * HD, (h + 1) * HD)

    def keys(buf, tile, group, h):
        slab = group if part == "first" else tile // TD + group
        rows = buf[pl.ds(slab * TD, TD), :, lanes(h)]
        return rows.reshape(TD * KEYS, HD)

    def is_live(tile, group, i):
        slab = tile // TD
        at = {"first": group + 1 - slab, "last": 2 * slab, "all": group}[part]
        return live_ref[tile, at * TD + i] > 0

    def score(tile, group, heads):
        for h in heads:
            scores = lax.dot_general(
                qbuf[tile, :, lanes(h)], keys(kbuf, tile, group, h),
                (((1,), (1,)), ((), ())), preferred_element_type=jnp.float32,
            ) * EXP_SCALE
            sbuf[h, group] = scores
            best = mbuf[h]
            for i in range(TD):
                top = functools.reduce(
                    jnp.maximum, [scores[:, lanes(i * 3 + g)] for g in range(3)]
                )
                best = jnp.maximum(best, jnp.where(is_live(tile, group, i), top, -1e30))
            mbuf[h] = best

    def weigh(tile, group, heads):
        for h in heads:
            best = mbuf[h]
            values = keys(vbuf, tile, group, h)
            for i in range(TD):
                top = jnp.where(is_live(tile, group, i), best, 1e30)
                parts = [jnp.exp2(sbuf[h, group, :, lanes(i * 3 + g)] - top) for g in range(3)]
                lbuf[h] += parts[0] + parts[1] + parts[2]
                abuf[h] += jnp.dot(
                    jnp.concatenate([p.astype(jnp.bfloat16) for p in parts], axis=-1),
                    values[i * KEYS : (i + 1) * KEYS], preferred_element_type=jnp.float32,
                )

    @pl.loop(0, 2 * TD)
    def _(tile):
        for h in range(nh):
            if carry is None:
                mbuf[h] = jnp.full(mbuf.shape[1:], -1e30, jnp.float32)
            else:
                mbuf[h] = carry[0][tile, h]

        for group in range(groups):
            score(tile, group, range(nh))

        for h in range(nh):
            top = jnp.max(mbuf[h], axis=-1, keepdims=True)
            mbuf[h] = jnp.broadcast_to(top, (ROWS, 128))
            if carry is None:
                lbuf[h] = jnp.zeros(lbuf.shape[1:], jnp.float32)
                abuf[h] = jnp.zeros(abuf.shape[1:], jnp.float32)
            else:
                scale = jnp.exp2(carry[0][tile, h] - mbuf[h])
                lbuf[h] = carry[1][tile, h] * scale
                abuf[h] = carry[2][tile, h] * scale

        for group in range(groups):
            weigh(tile, group, range(nh))

        for h in range(nh):
            if part == "first":
                outs[0][tile, h] = mbuf[h]
                outs[1][tile, h] = lbuf[h]
                outs[2][tile, h] = abuf[h]
            else:
                total = jnp.sum(lbuf[h], axis=-1, keepdims=True)
                result = (abuf[h] / total).astype(jnp.bfloat16)
                for u in range(4):
                    at = tile // TD * 4 + u
                    where = slice(base + h * HD, base + (h + 1) * HD)
                    outs[0][at, tile % TD, :, where] = result[u * LOC : (u + 1) * LOC]

    if early is not None:
        outs[0][:, :, :, :base] = early[...]


def attend(part, live, arrays, carry=(), early=()):
    width = arrays[0].shape[-1]
    nh = width // HD
    whole = pl.BlockSpec(memory_space=pltpu.VMEM)
    if part == "first":
        shapes = [jax.ShapeDtypeStruct((2 * TD, nh, ROWS, 128), jnp.float32)] * 3
    else:
        both = width + sum(block.shape[-1] for block in early)
        shapes = [jax.ShapeDtypeStruct((8, TD, LOC, both), jnp.bfloat16)]
    held = {"first": 2, "last": 2, "all": 4}[part] * TD
    return pl.pallas_call(
        functools.partial(attend_kernel, part, nh),
        in_specs=[pl.BlockSpec(memory_space=pltpu.SMEM)]
        + [pl.BlockSpec(memory_space=pl.ANY)] * len(arrays)
        + [whole] * (len(carry) + len(early)),
        out_specs=[whole] * len(shapes),
        out_shape=shapes,
        scratch_shapes=[
            pltpu.VMEM((2 * TD, ROWS, width), jnp.bfloat16),
            pltpu.VMEM((held, KEYS, width), jnp.bfloat16),
            pltpu.VMEM((held, KEYS, width), jnp.bfloat16),
            pltpu.VMEM((nh, SLABS[part], ROWS, TD * KEYS), jnp.float32),
            pltpu.VMEM((nh, ROWS, 128), jnp.float32),
            pltpu.VMEM((nh, ROWS, HD), jnp.float32),
            pltpu.VMEM((nh, ROWS, 128), jnp.float32),
            pltpu.SemaphoreType.DMA((72,)),
        ],
        compiler_params=pltpu.CompilerParams(vmem_limit_bytes=24 << 20),
    )(live, *arrays, *carry, *early)


def unpack_kernel(ref, out_ref):
    width = ref.shape[-1]
    for chip in range(8):
        out_ref[:, :, chip * width : (chip + 1) * width] = ref[chip]


def unpack(block):
    whole = pl.BlockSpec(memory_space=pltpu.VMEM)
    return pl.pallas_call(
        unpack_kernel,
        in_specs=[whole],
        out_specs=whole,
        out_shape=jax.ShapeDtypeStruct((TD, LOC, 24 * HD), jnp.bfloat16),
        name="unpack",
    )(block)


def compute(query_proj, key_proj, value_proj, query_gain, key_gain, neighbours, tile_counts):
    slab = lax.axis_index("ylo")
    column = lax.axis_index("z") * SIZES[3] + lax.axis_index("x")
    table = jnp.concatenate([neighbours, tile_counts[:, None]], axis=1)
    other = lax.ppermute(table, AXES, SWAP_SLAB)
    table = jnp.where(slab == 0, jnp.stack([table, other]), jnp.stack([other, table]))
    table = table.reshape(2 * TD, NB + 1)
    first_tile = (2 * column - 1) * TD + TD * (jnp.arange(2 * TD, dtype=jnp.int32) // TD)
    local = table[:, :NB] - first_tile[:, None]
    place = jnp.arange(NB, dtype=jnp.int32)
    counted = place[None, :] < table[:, NB:]
    match = (local[:, None, :] == place[None, :, None]) & counted[:, None, :]
    live = jnp.any(match, axis=2).astype(jnp.int32)

    early = ()
    for i, heads in enumerate(CHUNKS):
        block = pack(heads, query_proj, key_proj, value_proj, query_gain, key_gain)
        own = lax.all_to_all(block, RING, 0, 0, tiled=True)
        prev_own = lax.ppermute(own[4:, 1:], AXES, FORWARD)
        next_own = lax.ppermute(own[:4, 1:], AXES, BACKWARD)
        mate = lax.ppermute(own, AXES, SWAP_CORE)
        prev_mate = lax.ppermute(prev_own, AXES, SWAP_CORE)
        next_mate = lax.ppermute(next_own, AXES, SWAP_CORE)
        halo = [prev_own, prev_mate, next_own, next_mate]
        if i == len(CHUNKS) - 1:
            carry = attend("first", live, [own, mate])
            (done,) = attend("last", live, [own, *halo], carry, early)
        else:
            early = attend("all", live, [own, mate, *halo])
    done = lax.all_to_all(done, RING, 0, 0, tiled=True)
    return unpack(done)


def solution(mesh):
    split = Mesh(mesh.devices.reshape(SIZES), AXES)
    blk, uly = ("z", "x", "ylo"), ("yhi", "core")
    rows = P(blk, uly, None)
    in_specs = (rows, rows, rows, P(), P(), P(blk, None), P(blk))
    return jax.shard_map(compute, mesh=split, in_specs=in_specs, out_specs=rows, check_vma=False)
```

time: 199 us -> 183 us (0.920)
  the two profiles are of different devices: /device:TPU:198 before, /device:TPU:256 now
where the time goes in v1:
time: 183 us; the launch traced here: 182 us
  waiting for transfers between devices  60.3 us (33%)
  starting transfers between devices  44.2 us (24%)
  Pallas kernels  43.9 us (24%)
  blocking collectives  28.5 us (16%)
  local copies, waits for them, and re-layouts  3.96 us (2%)
    all_to_all x2, waiting for transfers between devices, compute(): own = lax.all_to_all(block, RING, 0, 0, tiled=True)  48.4 us
    pallas_call x3, Pallas kernels, attend(): pl.pallas_call(functools.partial(attend_kernel, part, nh), in_specs=[pl.B...  35.1 us
    all_to_all x1, blocking collectives, compute(): done = lax.all_to_all(done, RING, 0, 0, tiled=True)  28.5 us
    all_to_all x2, starting transfers between devices, compute(): own = lax.all_to_all(block, RING, 0, 0, tiled=True)  11.8 us
    ppermute x2, starting transfers between devices, compute(): next_own = lax.ppermute(own[:4, 1:], AXES, BACKWARD)  9.51 us
    ppermute x2, waiting for transfers between devices, compute(): prev_own = lax.ppermute(own[4:, 1:], AXES, FORWARD)  9.28 us
    pallas_call x2, Pallas kernels, pack(): pl.pallas_call(functools.partial(pack_kernel, heads), in_specs=[whole] *...  6.69 us
    ppermute x2, starting transfers between devices, compute(): prev_own = lax.ppermute(own[4:, 1:], AXES, FORWARD)  5.46 us
  transfers between devices with their start and end apart: 13, of which 5 were waited for; matrix products, arithmetic and copies ran while one was open for 2% of the time, Pallas kernels for 16%

profile of v1, /device:TPU:256, one launch (start us, length us, event | category | flops | bytes accessed | tf_op | source)
XLA Modules:
  0.0 181.7 jit_solution(924293553629247687)
XLA Ops:
  0.0 3.7 %shard_map.73 = bf16[8,3,3,48,256]{4,3,2,1,0:T(8,128)(2,1)} custom-call(bf16[3,48,3072]{2,1,0:T(8,128)(2,1)} %q_ref.3, bf16[3,48,3072]{2,1,0:T(8,128)(2,1)} %k_ref.3, bf16[3,48,3072]{2,1,0:T(8,128)(2,1)} %v_ref.3, f32[1,128]{1,0:T(1,128)} %bitcast.6, f32[1,128]{1,0:T(1,128)} %bitcast.8), custom_call_target="tpu_custom_call" | custom-call | tf_op jit(solution)/shard_map/pallas_call | solution.py:68
  3.7 7.1 %all-to-all-start = ((bf16[8,3,3,48,256]{4,3,2,1,0:T(8,128)(2,1)}), bf16[8,3,3,48,256]{4,3,2,1,0:T(8,128)(2,1)S(1)}, u32[]{:S(2)}, u32[]{:S(2)}) async-start(bf16[8,3,3,48,256]{4,3,2,1,0:T(8,128)(2,1)} %shard_map.73), calls=%async_computation | async-start | bytes 3538944 | tf_op jit(solution)/shard_map/all_to_all | solution.py:269
  10.8 3.0 %shard_map.75 = bf16[8,3,3,48,128]{4,3,2,1,0:T(8,128)(2,1)} custom-call(bf16[3,48,3072]{2,1,0:T(8,128)(2,1)} %q_ref.3, bf16[3,48,3072]{2,1,0:T(8,128)(2,1)} %k_ref.3, bf16[3,48,3072]{2,1,0:T(8,128)(2,1)} %v_ref.3, f32[1,128]{1,0:T(1,128)} %bitcast.7, f32[1,128]{1,0:T(1,128)} %bitcast.9), custom_call_target="tpu_custom_call" | custom-call | tf_op jit(solution)/shard_map/pallas_call | solution.py:68
  13.8 38.4 %all-to-all-done.refs_0_ = bf16[8,3,3,48,256]{4,3,2,1,0:T(8,128)(2,1)S(1)} async-done(((bf16[8,3,3,48,256]{4,3,2,1,0:T(8,128)(2,1)}), bf16[8,3,3,48,256]{4,3,2,1,0:T(8,128)(2,1)S(1)}, u32[]{:S(2)}, u32[]{:S(2)}) %all-to-all-start) | async-done | bytes 1769504 | tf_op jit(solution)/shard_map/all_to_all | solution.py:269
  52.2 4.7 %all-to-all-start.1 = ((bf16[8,3,3,48,128]{4,3,2,1,0:T(8,128)(2,1)}), bf16[8,3,3,48,128]{4,3,2,1,0:T(8,128)(2,1)S(1)}, u32[]{:S(2)}, u32[]{:S(2)}) async-start(bf16[8,3,3,48,128]{4,3,2,1,0:T(8,128)(2,1)} %shard_map.75), calls=%async_computation.1 | async-start | bytes 1769472 | tf_op jit(solution)/shard_map/all_to_all | solution.py:269
  56.9 2.1 %collective-permute-start.5 = (bf16[8,3,3,48,256]{4,3,2,1,0:T(8,128)(2,1)S(1)}, bf16[8,3,3,48,256]{4,3,2,1,0:T(8,128)(2,1)}, u32[]{:S(2)}, u32[]{:S(2)}) collective-permute-start(bf16[8,3,3,48,256]{4,3,2,1,0:T(8,128)(2,1)S(1)} %all-to-all-done.refs_0_), channel_id=1, source_target_pairs={{0,64},{1,65},{2,66},{3,67},{4,68},{5,69},{6,70},{7,71},{8,72},{9,... | collective-permute-start | bytes 5308424 | tf_op jit(solution)/shard_map/ppermute | solution.py:272
  60.1 3.4 %collective-permute-start.1 = (bf16[4,2,3,48,256]{4,3,2,1,0:T(8,128)(2,1)}, bf16[4,2,3,48,256]{4,3,2,1,0:T(8,128)(2,1)}, u32[]{:S(2)}, u32[]{:S(2)}) collective-permute-start(bf16[4,2,3,48,256]{4,3,2,1,0:T(8,128)(2,1)} %get-tuple-element.12), channel_id=1, source_target_pairs={{0,2},{1,3},{2,4},{3,5},{4,6},{5,7},{6,8},{7,9},{8,10},{9,11},{10,... | collective-permute-start | bytes 1769480 | tf_op jit(solution)/shard_map/ppermute | solution.py:270
  63.5 5.8 %collective-permute-start.3 = (bf16[4,2,3,48,256]{4,3,2,1,0:T(8,128)(2,1)}, bf16[4,2,3,48,256]{4,3,2,1,0:T(8,128)(2,1)}, u32[]{:S(2)}, u32[]{:S(2)}) collective-permute-start(bf16[4,2,3,48,256]{4,3,2,1,0:T(8,128)(2,1)} %get-tuple-element.11), channel_id=1, source_target_pairs={{2,0},{3,1},{4,2},{5,3},{6,4},{7,5},{8,6},{9,7},{10,8},{11,9},{12,... | collective-permute-start | bytes 1769480 | tf_op jit(solution)/shard_map/ppermute | solution.py:271
  69.3 10.0 %all-to-all-done.1.refs_0_ = bf16[8,3,3,48,128]{4,3,2,1,0:T(8,128)(2,1)S(1)} async-done(((bf16[8,3,3,48,128]{4,3,2,1,0:T(8,128)(2,1)}), bf16[8,3,3,48,128]{4,3,2,1,0:T(8,128)(2,1)S(1)}, u32[]{:S(2)}, u32[]{:S(2)}) %all-to-all-start.1) | async-done | bytes 884768 | tf_op jit(solution)/shard_map/all_to_all | solution.py:269
  80.0 3.7 %collective-permute-start.9 = (bf16[4,2,3,48,128]{4,3,2,1,0:T(8,128)(2,1)S(1)}, bf16[4,2,3,48,128]{4,3,2,1,0:T(8,128)(2,1)}, u32[]{:S(2)}, u32[]{:S(2)}) collective-permute-start(bf16[4,2,3,48,128]{4,3,2,1,0:T(8,128)(2,1)S(1)} %get-tuple-element.13), channel_id=1, source_target_pairs={{2,0},{3,1},{4,2},{5,3},{6,4},{7,5},{8,6},{9,7},{10,8},{11,9},{12,... | collective-permute-start | bytes 884744 | tf_op jit(solution)/shard_map/ppermute | solution.py:271
  83.9 4.9 %collective-permute-start = (s32[3,10]{1,0:T(4,128)S(1)}, s32[3,10]{1,0:T(4,128)S(1)}, u32[]{:S(2)}, u32[]{:S(2)}) collective-permute-start(s32[3,10]{1,0:T(4,128)S(1)} %pad_add_fusion), channel_id=1, source_target_pairs={{0,1},{1,0},{2,3},{3,2},{4,5},{5,4},{6,7},{7,6},{8,9},{9,8},{10,11... | collective-permute-start | bytes 368 | tf_op jit(solution)/shard_map/ppermute | solution.py:256
  88.8 1.5 collective-permute-done
  90.4 2.1 %collective-permute-start.7 = (bf16[4,2,3,48,128]{4,3,2,1,0:T(8,128)(2,1)}, bf16[4,2,3,48,128]{4,3,2,1,0:T(8,128)(2,1)}, u32[]{:S(2)}, u32[]{:S(2)}) collective-permute-start(bf16[4,2,3,48,128]{4,3,2,1,0:T(8,128)(2,1)} %get-tuple-element.14), channel_id=1, source_target_pairs={{0,2},{1,3},{2,4},{3,5},{4,6},{5,7},{6,8},{7,9},{8,10},{9,11},{10,... | collective-permute-start | bytes 884744 | tf_op jit(solution)/shard_map/ppermute | solution.py:270
  92.5 1.9 %collective-permute-start.6 = (bf16[8,3,3,48,128]{4,3,2,1,0:T(8,128)(2,1)S(1)}, bf16[8,3,3,48,128]{4,3,2,1,0:T(8,128)(2,1)S(1)}, u32[]{:S(2)}, u32[]{:S(2)}) collective-permute-start(bf16[8,3,3,48,128]{4,3,2,1,0:T(8,128)(2,1)S(1)} %all-to-all-done.1.refs_0_), channel_id=1, source_target_pairs={{0,64},{1,65},{2,66},{3,67},{4,68},{5,69},{6,70},{7,71},{8,72},{9,... | collective-permute-start | bytes 2654216 | tf_op jit(solution)/shard_map/ppermute | solution.py:272
  94.5 9.3 %collective-permute-done.7.refs_2_ = bf16[4,2,3,48,128]{4,3,2,1,0:T(8,128)(2,1)} collective-permute-done((bf16[4,2,3,48,128]{4,3,2,1,0:T(8,128)(2,1)}, bf16[4,2,3,48,128]{4,3,2,1,0:T(8,128)(2,1)}, u32[]{:S(2)}, u32[]{:S(2)}) %collective-permute-start.7) | collective-permute-done | bytes 294944 | tf_op jit(solution)/shard_map/ppermute | solution.py:270
  103.8 1.9 %collective-permute-start.10 = (bf16[4,2,3,48,128]{4,3,2,1,0:T(8,128)(2,1)}, bf16[4,2,3,48,128]{4,3,2,1,0:T(8,128)(2,1)S(1)}, u32[]{:S(2)}, u32[]{:S(2)}) collective-permute-start(bf16[4,2,3,48,128]{4,3,2,1,0:T(8,128)(2,1)} %collective-permute-done.9.refs_4_), channel_id=1, source_target_pairs={{0,64},{1,65},{2,66},{3,67},{4,68},{5,69},{6,70},{7,71},{8,72},{9,... | collective-permute-start | bytes 884744 | tf_op jit(solution)/shard_map/ppermute | solution.py:274
  105.7 2.4 %collective-permute-start.2 = (bf16[4,2,3,48,256]{4,3,2,1,0:T(8,128)(2,1)}, bf16[4,2,3,48,256]{4,3,2,1,0:T(8,128)(2,1)}, u32[]{:S(2)}, u32[]{:S(2)}) collective-permute-start(bf16[4,2,3,48,256]{4,3,2,1,0:T(8,128)(2,1)} %collective-permute-done.1.refs_1_), channel_id=1, source_target_pairs={{0,64},{1,65},{2,66},{3,67},{4,68},{5,69},{6,70},{7,71},{8,72},{9,... | collective-permute-start | bytes 1769480 | tf_op jit(solution)/shard_map/ppermute | solution.py:273
  108.1 1.9 %collective-permute-start.4 = (bf16[4,2,3,48,256]{4,3,2,1,0:T(8,128)(2,1)}, bf16[4,2,3,48,256]{4,3,2,1,0:T(8,128)(2,1)}, u32[]{:S(2)}, u32[]{:S(2)}) collective-permute-start(bf16[4,2,3,48,256]{4,3,2,1,0:T(8,128)(2,1)} %collective-permute-done.3.refs_3_), channel_id=1, source_target_pairs={{0,64},{1,65},{2,66},{3,67},{4,68},{5,69},{6,70},{7,71},{8,72},{9,... | collective-permute-start | bytes 1769480 | tf_op jit(solution)/shard_map/ppermute | solution.py:274
  111.0 2.4 %collective-permute-start.8 = (bf16[4,2,3,48,128]{4,3,2,1,0:T(8,128)(2,1)}, bf16[4,2,3,48,128]{4,3,2,1,0:T(8,128)(2,1)}, u32[]{:S(2)}, u32[]{:S(2)}) collective-permute-start(bf16[4,2,3,48,128]{4,3,2,1,0:T(8,128)(2,1)} %collective-permute-done.7.refs_2_), channel_id=1, source_target_pairs={{0,64},{1,65},{2,66},{3,67},{4,68},{5,69},{6,70},{7,71},{8,72},{9,... | collective-permute-start | bytes 884744 | tf_op jit(solution)/shard_map/ppermute | solution.py:273
  115.9 11.5 %shard_map.76.refs_8_ = bf16[8,3,48,128]{3,2,1,0:T(8,128)(2,1)S(1)} custom-call(s32[6,9]{1,0:T(8,128)S(1)} %convert_element_type.3.live_ref, bf16[8,3,3,48,128]{4,3,2,1,0:T(8,128)(2,1)S(1)} %all-to-all-done.1.refs_0_, bf16[8,3,3,48,128]{4,3,2,1,0:T(8,128)(2,1)S(1)} %collective-permute-done.6.refs_1_, ...), custom_call_target="tpu_custom_call" | custom-call | tf_op jit(solution)/shard_map/pallas_call | solution.py:214
  127.5 13.8 %shard_map.74 = (f32[6,2,192,128]{3,2,1,0:T(8,128)S(1)}, f32[6,2,192,128]{3,2,1,0:T(8,128)S(1)}, f32[6,2,192,128]{3,2,1,0:T(8,128)S(1)}) custom-call(s32[6,9]{1,0:T(8,128)S(1)} %convert_element_type.3.live_ref, bf16[8,3,3,48,256]{4,3,2,1,0:T(8,128)(2,1)S(1)} %all-to-all-done.refs_0_, bf16[8,3,3,48,256]{4,3,2,1,0:T(8,128)(2,1)} %collective-permute-done.5.refs_1_), custom_call_target="tpu_custom_call" | custom-call | tf_op jit(solution)/shard_map/pallas_call | solution.py:214
  141.3 9.8 %shard_map.77 = bf16[8,3,48,384]{3,2,1,0:T(8,128)(2,1)S(1)} custom-call(s32[6,9]{1,0:T(8,128)S(1)} %convert_element_type.3.live_ref, bf16[8,3,3,48,256]{4,3,2,1,0:T(8,128)(2,1)S(1)} %all-to-all-done.refs_0_, bf16[4,2,3,48,256]{4,3,2,1,0:T(8,128)(2,1)} %collective-permute-done.1.refs_1_, bf16[4,2,3,48,256]{4,3,2,1,0:T(8,128)(2,1)} %collective-permute-done.2.refs_2_, ...), custom_call_target="tpu_custom_call" | custom-call | tf_op jit(solution)/shard_map/pallas_call | solution.py:214
  151.1 28.5 %all_to_all.15.ref = bf16[8,3,48,384]{3,2,1,0:T(8,128)(2,1)} all-to-all(bf16[8,3,48,384]{3,2,1,0:T(8,128)(2,1)S(1)} %shard_map.77), channel_id=1, replica_groups=mesh['yhi'=4,'core'=2,'z'=8,'x'=4,'ylo'=2] {'ylo','yhi'}, dimensions={0} | all-to-all | bytes 1769472 | tf_op jit(solution)/shard_map/all_to_all | solution.py:281
  179.6 2.2 %unpack.1 = bf16[3,48,3072]{2,1,0:T(8,128)(2,1)} custom-call(bf16[8,3,48,384]{3,2,1,0:T(8,128)(2,1)} %all_to_all.15.ref), custom_call_target="tpu_custom_call" | custom-call | tf_op jit(solution)/shard_map/unpack/pallas_call | solution.py:243
  (31 shorter events, 5.6 us)
Async XLA Ops:
  3.7 48.6 %all-to-all-start = ((bf16[8,3,3,48,256]{4,3,2,1,0:T(8,128)(2,1)}), bf16[8,3,3,48,256]{4,3,2,1,0:T(8,128)(2,1)S(1)}, u32[]{:S(2)}, u32[]{:S(2)}) async-start(bf16[8,3,3,48,256]{4,3,2,1,0:T(8,128)(2,1)} %shard_map.73), calls=%async_computation | async-start | bytes 3538944 | tf_op jit(solution)/shard_map/all_to_all | solution.py:269
  52.2 27.0 %all-to-all-start.1 = ((bf16[8,3,3,48,128]{4,3,2,1,0:T(8,128)(2,1)}), bf16[8,3,3,48,128]{4,3,2,1,0:T(8,128)(2,1)S(1)}, u32[]{:S(2)}, u32[]{:S(2)}) async-start(bf16[8,3,3,48,128]{4,3,2,1,0:T(8,128)(2,1)} %shard_map.75), calls=%async_computation.1 | async-start | bytes 1769472 | tf_op jit(solution)/shard_map/all_to_all | solution.py:269
  56.9 26.9 %copy-start.3 = (s32[3]{0:T(128)S(1)}, s32[3]{0:T(128)}, u32[]{:S(2)}) copy-start(s32[3]{0:T(128)} %param.13) | copy-start | bytes 40
  56.9 27.0 %copy-start.2 = (s32[3,9]{1,0:T(4,128)S(1)}, s32[3,9]{1,0:T(4,128)}, u32[]{:S(2)}) copy-start(s32[3,9]{1,0:T(4,128)} %param.12) | copy-start | bytes 328
  56.9 70.6 %collective-permute-start.5 = (bf16[8,3,3,48,256]{4,3,2,1,0:T(8,128)(2,1)S(1)}, bf16[8,3,3,48,256]{4,3,2,1,0:T(8,128)(2,1)}, u32[]{:S(2)}, u32[]{:S(2)}) collective-permute-start(bf16[8,3,3,48,256]{4,3,2,1,0:T(8,128)(2,1)S(1)} %all-to-all-done.refs_0_), channel_id=1, source_target_pairs={{0,64},{1,65},{2,66},{3,67},{4,68},{5,69},{6,70},{7,71},{8,72},{9,... | collective-permute-start | bytes 5308424 | tf_op jit(solution)/shard_map/ppermute | solution.py:272
  60.1 45.6 %collective-permute-start.1 = (bf16[4,2,3,48,256]{4,3,2,1,0:T(8,128)(2,1)}, bf16[4,2,3,48,256]{4,3,2,1,0:T(8,128)(2,1)}, u32[]{:S(2)}, u32[]{:S(2)}) collective-permute-start(bf16[4,2,3,48,256]{4,3,2,1,0:T(8,128)(2,1)} %get-tuple-element.12), channel_id=1, source_target_pairs={{0,2},{1,3},{2,4},{3,5},{4,6},{5,7},{6,8},{7,9},{8,10},{9,11},{10,... | collective-permute-start | bytes 1769480 | tf_op jit(solution)/shard_map/ppermute | solution.py:270
  63.5 44.6 %collective-permute-start.3 = (bf16[4,2,3,48,256]{4,3,2,1,0:T(8,128)(2,1)}, bf16[4,2,3,48,256]{4,3,2,1,0:T(8,128)(2,1)}, u32[]{:S(2)}, u32[]{:S(2)}) collective-permute-start(bf16[4,2,3,48,256]{4,3,2,1,0:T(8,128)(2,1)} %get-tuple-element.11), channel_id=1, source_target_pairs={{2,0},{3,1},{4,2},{5,3},{6,4},{7,5},{8,6},{9,7},{10,8},{11,9},{12,... | collective-permute-start | bytes 1769480 | tf_op jit(solution)/shard_map/ppermute | solution.py:271
  80.0 12.5 %collective-permute-start.9 = (bf16[4,2,3,48,128]{4,3,2,1,0:T(8,128)(2,1)S(1)}, bf16[4,2,3,48,128]{4,3,2,1,0:T(8,128)(2,1)}, u32[]{:S(2)}, u32[]{:S(2)}) collective-permute-start(bf16[4,2,3,48,128]{4,3,2,1,0:T(8,128)(2,1)S(1)} %get-tuple-element.13), channel_id=1, source_target_pairs={{2,0},{3,1},{4,2},{5,3},{6,4},{7,5},{8,6},{9,7},{10,8},{11,9},{12,... | collective-permute-start | bytes 884744 | tf_op jit(solution)/shard_map/ppermute | solution.py:271
  83.9 6.4 %collective-permute-start = (s32[3,10]{1,0:T(4,128)S(1)}, s32[3,10]{1,0:T(4,128)S(1)}, u32[]{:S(2)}, u32[]{:S(2)}) collective-permute-start(s32[3,10]{1,0:T(4,128)S(1)} %pad_add_fusion), channel_id=1, source_target_pairs={{0,1},{1,0},{2,3},{3,2},{4,5},{5,4},{6,7},{7,6},{8,9},{9,8},{10,11... | collective-permute-start | bytes 368 | tf_op jit(solution)/shard_map/ppermute | solution.py:256
  90.4 13.4 %collective-permute-start.7 = (bf16[4,2,3,48,128]{4,3,2,1,0:T(8,128)(2,1)}, bf16[4,2,3,48,128]{4,3,2,1,0:T(8,128)(2,1)}, u32[]{:S(2)}, u32[]{:S(2)}) collective-permute-start(bf16[4,2,3,48,128]{4,3,2,1,0:T(8,128)(2,1)} %get-tuple-element.14), channel_id=1, source_target_pairs={{0,2},{1,3},{2,4},{3,5},{4,6},{5,7},{6,8},{7,9},{8,10},{9,11},{10,... | collective-permute-start | bytes 884744 | tf_op jit(solution)/shard_map/ppermute | solution.py:270
  92.5 22.4 %collective-permute-start.6 = (bf16[8,3,3,48,128]{4,3,2,1,0:T(8,128)(2,1)S(1)}, bf16[8,3,3,48,128]{4,3,2,1,0:T(8,128)(2,1)S(1)}, u32[]{:S(2)}, u32[]{:S(2)}) collective-permute-start(bf16[8,3,3,48,128]{4,3,2,1,0:T(8,128)(2,1)S(1)} %all-to-all-done.1.refs_0_), channel_id=1, source_target_pairs={{0,64},{1,65},{2,66},{3,67},{4,68},{5,69},{6,70},{7,71},{8,72},{9,... | collective-permute-start | bytes 2654216 | tf_op jit(solution)/shard_map/ppermute | solution.py:272
  103.8 6.5 %collective-permute-start.10 = (bf16[4,2,3,48,128]{4,3,2,1,0:T(8,128)(2,1)}, bf16[4,2,3,48,128]{4,3,2,1,0:T(8,128)(2,1)S(1)}, u32[]{:S(2)}, u32[]{:S(2)}) collective-permute-start(bf16[4,2,3,48,128]{4,3,2,1,0:T(8,128)(2,1)} %collective-permute-done.9.refs_4_), channel_id=1, source_target_pairs={{0,64},{1,65},{2,66},{3,67},{4,68},{5,69},{6,70},{7,71},{8,72},{9,... | collective-permute-start | bytes 884744 | tf_op jit(solution)/shard_map/ppermute | solution.py:274
  105.7 35.6 %collective-permute-start.2 = (bf16[4,2,3,48,256]{4,3,2,1,0:T(8,128)(2,1)}, bf16[4,2,3,48,256]{4,3,2,1,0:T(8,128)(2,1)}, u32[]{:S(2)}, u32[]{:S(2)}) collective-permute-start(bf16[4,2,3,48,256]{4,3,2,1,0:T(8,128)(2,1)} %collective-permute-done.1.refs_1_), channel_id=1, source_target_pairs={{0,64},{1,65},{2,66},{3,67},{4,68},{5,69},{6,70},{7,71},{8,72},{9,... | collective-permute-start | bytes 1769480 | tf_op jit(solution)/shard_map/ppermute | solution.py:273
  108.1 33.2 %collective-permute-start.4 = (bf16[4,2,3,48,256]{4,3,2,1,0:T(8,128)(2,1)}, bf16[4,2,3,48,256]{4,3,2,1,0:T(8,128)(2,1)}, u32[]{:S(2)}, u32[]{:S(2)}) collective-permute-start(bf16[4,2,3,48,256]{4,3,2,1,0:T(8,128)(2,1)} %collective-permute-done.3.refs_3_), channel_id=1, source_target_pairs={{0,64},{1,65},{2,66},{3,67},{4,68},{5,69},{6,70},{7,71},{8,72},{9,... | collective-permute-start | bytes 1769480 | tf_op jit(solution)/shard_map/ppermute | solution.py:274
  110.3 0.7 copy-start
  111.0 3.9 %collective-permute-start.8 = (bf16[4,2,3,48,128]{4,3,2,1,0:T(8,128)(2,1)}, bf16[4,2,3,48,128]{4,3,2,1,0:T(8,128)(2,1)}, u32[]{:S(2)}, u32[]{:S(2)}) collective-permute-start(bf16[4,2,3,48,128]{4,3,2,1,0:T(8,128)(2,1)} %collective-permute-done.7.refs_2_), channel_id=1, source_target_pairs={{0,64},{1,65},{2,66},{3,67},{4,68},{5,69},{6,70},{7,71},{8,72},{9,... | collective-permute-start | bytes 884744 | tf_op jit(solution)/shard_map/ppermute | solution.py:273
  115.0 1.0 copy-start.1

commit v2 on v1

v2 whole, which is shorter than its diff:
```python
import functools
import math

import jax
import jax.numpy as jnp
import numpy as np
from jax import lax
from jax.experimental import pallas as pl
from jax.experimental.pallas import tpu as pltpu
from jax.sharding import Mesh
from jax.sharding import PartitionSpec as P


HD = 128
NB = 9
TD = 3
LOC = 48
COLS = 8 * 4
SIZES = (4, 2, 8, 4, 2)
AXES = ("yhi", "core", "z", "x", "ylo")
RING = ("ylo", "yhi")
HEADS = 3
ROWS = 4 * LOC
KEYS = 8 * LOC
SLABS = {"first": 2, "last": 1}
EXP_SCALE = math.log2(math.e) / math.sqrt(HD)


def route(move):
    pairs = []
    for i, at in enumerate(np.ndindex(*SIZES)):
        to = move(*at)
        if to is not None:
            pairs.append((i, int(np.ravel_multi_index(to, SIZES))))
    return pairs


def to_column(distance):
    def move(u, c, z, x, p):
        n = z * 4 + x + distance
        return (u, c, n // 4, n % 4, p) if 0 <= n < COLS else None

    return route(move)


SWAP_CORE = route(lambda u, c, z, x, p: (u, 1 - c, z, x, p))
SWAP_SLAB = route(lambda u, c, z, x, p: (u, c, z, x, 1 - p))
FORWARD = to_column(1)
BACKWARD = to_column(-1)


def pack_kernel(normed, *refs):
    out_ref = refs[-1]
    refs = list(refs[:-1])
    for which, has_gain in enumerate(normed):
        ref = refs.pop(0)
        gain = refs.pop(0) if has_gain else None
        for chip in range(8):
            for head in range(HEADS):
                at = (chip * HEADS + head) * HD
                part = ref[:, :, at : at + HD]
                if has_gain:
                    wide = part.astype(jnp.float32)
                    mean = jnp.mean(wide * wide, axis=-1, keepdims=True)
                    part = (wide * lax.rsqrt(mean + 1e-06) * gain[...]).astype(jnp.bfloat16)
                out_ref[chip, which, :, :, head * HD : (head + 1) * HD] = part


def pack(*pairs):
    whole = pl.BlockSpec(memory_space=pltpu.VMEM)
    operands = []
    for array, gain in pairs:
        operands += [array] if gain is None else [array, gain.reshape(1, HD)]
    shape = (8, len(pairs), TD, LOC, HEADS * HD)
    return pl.pallas_call(
        functools.partial(pack_kernel, [gain is not None for _, gain in pairs]),
        in_specs=[whole] * len(operands),
        out_specs=whole,
        out_shape=jax.ShapeDtypeStruct(shape, jnp.bfloat16),
    )(*operands)


def attend_kernel(part, nh, live_ref, query, *refs):
    refs = list(refs)
    lbuf, abuf, mbuf, sbuf = (refs.pop() for _ in range(4))
    column = (refs.pop(0), refs.pop(0)) if part == "first" else None
    before = (refs.pop(0), refs.pop(0)) if part == "last" else None
    after = (refs.pop(0), refs.pop(0)) if part == "last" else None
    carry = [refs.pop(0) for _ in range(3)] if part == "last" else None
    outs = refs

    def lanes(h):
        return slice(h * HD, (h + 1) * HD)

    def slabs(p):
        if part == "first":
            return [(column, 0, 1 - p), (column, 4, 2 - p)]
        return [(before, 0, 0)] if p == 0 else [(after, 0, 2)]

    def key_tile(slab, kv, t, h):
        arrays, first, _ = slab
        pieces = [a[first + u, kv, t, :, lanes(h)] for a in arrays for u in range(4)]
        return jnp.concatenate(pieces, axis=0)

    def query_tile(p, t, h):
        return jnp.concatenate([query[p * 4 + u, 0, t, :, lanes(h)] for u in range(4)], axis=0)

    def score(p, t, group, slab, h):
        keys = jnp.concatenate([key_tile(slab, 0, i, h) for i in range(TD)], axis=0)
        scores = lax.dot_general(
            query_tile(p, t, h), keys,
            (((1,), (1,)), ((), ())), preferred_element_type=jnp.float32,
        ) * EXP_SCALE
        sbuf[h, group] = scores
        best = mbuf[h]
        for i in range(TD):
            live = live_ref[p * TD + t, slab[2] * TD + i] > 0
            top = functools.reduce(jnp.maximum, [scores[:, lanes(i * 3 + g)] for g in range(3)])
            best = jnp.maximum(best, jnp.where(live, top, -1e30))
        mbuf[h] = best

    def weigh(p, t, group, slab, h):
        best = mbuf[h]
        for i in range(TD):
            live = live_ref[p * TD + t, slab[2] * TD + i] > 0
            top = jnp.where(live, best, 1e30)
            parts = [jnp.exp2(sbuf[h, group, :, lanes(i * 3 + g)] - top) for g in range(3)]
            lbuf[h] += parts[0] + parts[1] + parts[2]
            abuf[h] += jnp.dot(
                jnp.concatenate([w.astype(jnp.bfloat16) for w in parts], axis=-1),
                key_tile(slab, 1, i, h), preferred_element_type=jnp.float32,
            )

    def attend_tile(p, t):
        tile = p * TD + t
        for h in range(nh):
            if carry is None:
                mbuf[h] = jnp.full(mbuf.shape[1:], -1e30, jnp.float32)
            else:
                mbuf[h] = carry[0][tile, h]
        for group, slab in enumerate(slabs(p)):
            for h in range(nh):
                score(p, t, group, slab, h)
        for h in range(nh):
            top = jnp.max(mbuf[h], axis=-1, keepdims=True)
            mbuf[h] = jnp.broadcast_to(top, (ROWS, 128))
            if carry is None:
                lbuf[h] = jnp.zeros(lbuf.shape[1:], jnp.float32)
                abuf[h] = jnp.zeros(abuf.shape[1:], jnp.float32)
            else:
                scale = jnp.exp2(carry[0][tile, h] - mbuf[h])
                lbuf[h] = carry[1][tile, h] * scale
                abuf[h] = carry[2][tile, h] * scale
        for group, slab in enumerate(slabs(p)):
            for h in range(nh):
                weigh(p, t, group, slab, h)
        for h in range(nh):
            if part == "first":
                outs[0][tile, h] = mbuf[h]
                outs[1][tile, h] = lbuf[h]
                outs[2][tile, h] = abuf[h]
            else:
                total = jnp.sum(lbuf[h], axis=-1, keepdims=True)
                result = (abuf[h] / total).astype(jnp.bfloat16)
                for u in range(4):
                    outs[0][p * 4 + u, t, :, lanes(h)] = result[u * LOC : (u + 1) * LOC]

    for p in range(2):

        @pl.loop(0, TD)
        def _(t):
            attend_tile(p, t)


def attend(part, live, arrays, carry=()):
    width = arrays[0].shape[-1]
    nh = width // HD
    whole = pl.BlockSpec(memory_space=pltpu.VMEM)
    if part == "first":
        shapes = [jax.ShapeDtypeStruct((2 * TD, nh, ROWS, 128), jnp.float32)] * 3
    else:
        shapes = [jax.ShapeDtypeStruct((8, TD, LOC, width), jnp.bfloat16)]
    return pl.pallas_call(
        functools.partial(attend_kernel, part, nh),
        in_specs=[pl.BlockSpec(memory_space=pltpu.SMEM)]
        + [whole] * (len(arrays) + len(carry)),
        out_specs=[whole] * len(shapes),
        out_shape=shapes,
        scratch_shapes=[
            pltpu.VMEM((nh, SLABS[part], ROWS, TD * KEYS), jnp.float32),
            pltpu.VMEM((nh, ROWS, 128), jnp.float32),
            pltpu.VMEM((nh, ROWS, HD), jnp.float32),
            pltpu.VMEM((nh, ROWS, 128), jnp.float32),
        ],
        compiler_params=pltpu.CompilerParams(vmem_limit_bytes=32 << 20),
    )(live, *arrays, *carry)


def unpack_kernel(ref, out_ref):
    width = ref.shape[-1]
    for chip in range(8):
        out_ref[:, :, chip * width : (chip + 1) * width] = ref[chip]


def unpack(block):
    whole = pl.BlockSpec(memory_space=pltpu.VMEM)
    return pl.pallas_call(
        unpack_kernel,
        in_specs=[whole],
        out_specs=whole,
        out_shape=jax.ShapeDtypeStruct((TD, LOC, 24 * HD), jnp.bfloat16),
        name="unpack",
    )(block)


def compute(query_proj, key_proj, value_proj, query_gain, key_gain, neighbours, tile_counts):
    slab = lax.axis_index("ylo")
    column = lax.axis_index("z") * SIZES[3] + lax.axis_index("x")
    table = jnp.concatenate([neighbours, tile_counts[:, None]], axis=1)
    other = lax.ppermute(table, AXES, SWAP_SLAB)
    table = jnp.where(slab == 0, jnp.stack([table, other]), jnp.stack([other, table]))
    table = table.reshape(2 * TD, NB + 1)
    first_tile = (2 * column - 1) * TD + TD * (jnp.arange(2 * TD, dtype=jnp.int32) // TD)
    local = table[:, :NB] - first_tile[:, None]
    place = jnp.arange(NB, dtype=jnp.int32)
    counted = place[None, :] < table[:, NB:]
    match = (local[:, None, :] == place[None, :, None]) & counted[:, None, :]
    live = jnp.any(match, axis=2).astype(jnp.int32)

    block = pack((key_proj, key_gain), (value_proj, None))
    own = lax.all_to_all(block, RING, 0, 0, tiled=True)
    block = pack((query_proj, query_gain))
    query = lax.all_to_all(block, RING, 0, 0, tiled=True)
    prev_own = lax.ppermute(own[4:], AXES, FORWARD)
    next_own = lax.ppermute(own[:4], AXES, BACKWARD)
    mate = lax.ppermute(own, AXES, SWAP_CORE)
    prev_mate = lax.ppermute(prev_own, AXES, SWAP_CORE)
    next_mate = lax.ppermute(next_own, AXES, SWAP_CORE)
    carry = attend("first", live, [query, own, mate])
    halo = [prev_own, prev_mate, next_own, next_mate]
    (done,) = attend("last", live, [query, *halo], carry)
    done = lax.all_to_all(done, RING, 0, 0, tiled=True)
    return unpack(done)


def solution(mesh):
    split = Mesh(mesh.devices.reshape(SIZES), AXES)
    blk, uly = ("z", "x", "ylo"), ("yhi", "core")
    rows = P(blk, uly, None)
    in_specs = (rows, rows, rows, P(), P(), P(blk, None), P(blk))
    return jax.shard_map(compute, mesh=split, in_specs=in_specs, out_specs=rows, check_vma=False)
```

time: 183 us -> 148 us (0.81)
  blocking collectives: 28.5 us -> 79 us
  waiting for transfers between devices: 60.3 us -> 13.5 us
  starting transfers between devices: 44.2 us -> 22.9 us
  Pallas kernels: 43.9 us -> 29.4 us
  local copies, waits for them, and re-layouts: 3.96 us -> 1.8 us
    all_to_all x0 -> x1, blocking collectives: none -> 49.7 us  [compute(): own = lax.all_to_all(block, RING, 0, 0, tiled=True)]
    all_to_all x2 -> x1, waiting for transfers between devices: 48.4 us -> 0.1 us  [compute(): query = lax.all_to_all(block, RING, 0, 0, tiled=True)]
    pallas_call x3 -> x2, Pallas kernels: 35.1 us -> 21.3 us  [attend(): pl.pallas_call(functools.partial(attend_kernel, part, nh), in_specs=[pl.B...]
    ppermute x1, waiting for transfers between devices: 1.54 us -> 11.9 us  [compute(): other = lax.ppermute(table, AXES, SWAP_SLAB)]
    all_to_all x2 -> x1, starting transfers between devices: 11.8 us -> 3.55 us  [compute(): query = lax.all_to_all(block, RING, 0, 0, tiled=True)]
    ppermute x4 -> x2, waiting for transfers between devices: 9.29 us -> 1.44 us  [the longest x1 1.44 us: compute(): prev_own = lax.ppermute(own[4:], AXES, FORWARD)]
    ppermute x4 -> x2, starting transfers between devices: 15 us -> 9.15 us  [the longest x1 5.76 us: compute(): next_own = lax.ppermute(own[:4], AXES, BACKWARD)]
    ppermute x2 -> x1, starting transfers between devices: 4.8 us -> 1.91 us  [compute(): prev_mate = lax.ppermute(prev_own, AXES, SWAP_CORE)]
  transfers between devices with their start and end apart: 13 -> 7, of which waited for: 5 -> 3; matrix products, arithmetic and copies ran while one was open for 2% -> 1% of each run, Pallas kernels for 16% -> 10%
where the time goes in v2:
time: 148 us
  blocking collectives  79 us (53%)
  Pallas kernels  29.4 us (20%)
  starting transfers between devices  22.9 us (15%)
  waiting for transfers between devices  13.5 us (9%)
  local copies, waits for them, and re-layouts  1.8 us (1%)
    all_to_all x1, blocking collectives, compute(): own = lax.all_to_all(block, RING, 0, 0, tiled=True)  49.7 us
    all_to_all x1, blocking collectives, compute(): done = lax.all_to_all(done, RING, 0, 0, tiled=True)  29.3 us
    pallas_call x2, Pallas kernels, attend(): pl.pallas_call(functools.partial(attend_kernel, part, nh), in_specs=[pl.B...  21.3 us
    ppermute x1, waiting for transfers between devices, compute(): other = lax.ppermute(table, AXES, SWAP_SLAB)  11.9 us
    pallas_call x2, Pallas kernels, pack(): pl.pallas_call(functools.partial(pack_kernel, [gain is not None for _, ga...  5.9 us
    ppermute x1, starting transfers between devices, compute(): next_own = lax.ppermute(own[:4], AXES, BACKWARD)  5.76 us
    ppermute x1, starting transfers between devices, compute(): other = lax.ppermute(table, AXES, SWAP_SLAB)  3.97 us
    all_to_all x1, starting transfers between devices, compute(): query = lax.all_to_all(block, RING, 0, 0, tiled=True)  3.55 us
  transfers between devices with their start and end apart: 7, of which 3 were waited for; matrix products, arithmetic and copies ran while one was open for 1% of the time, Pallas kernels for 10%

profile of v2, /device:TPU:256, one launch (start us, length us, event | category | flops | bytes accessed | tf_op | source)
XLA Modules:
  0.0 147.9 jit_solution(4353912706259945654)
XLA Ops:
  0.0 3.3 %shard_map.74 = bf16[8,2,3,48,384]{4,3,2,1,0:T(8,128)(2,1)} custom-call(bf16[3,48,3072]{2,1,0:T(8,128)(2,1)} %refs_0_.3, f32[1,128]{1,0:T(1,128)} %bitcast.9, bf16[3,48,3072]{2,1,0:T(8,128)(2,1)} %refs_2_.1), custom_call_target="tpu_custom_call" | custom-call | tf_op jit(solution)/shard_map/pallas_call | solution.py:75
  3.3 49.7 %all_to_all.15.refs_0_ = bf16[8,2,3,48,384]{4,3,2,1,0:T(8,128)(2,1)S(1)} all-to-all(bf16[8,2,3,48,384]{4,3,2,1,0:T(8,128)(2,1)} %shard_map.74), channel_id=1, replica_groups=mesh['yhi'=4,'core'=2,'z'=8,'x'=4,'ylo'=2] {'ylo','yhi'}, dimensions={0} | all-to-all | bytes 3538944 | tf_op jit(solution)/shard_map/all_to_all | solution.py:231
  53.0 1.4 fusion.4
  54.4 3.4 %collective-permute-start.1 = (bf16[4,2,3,48,384]{4,3,2,1,0:T(8,128)(2,1)}, bf16[4,2,3,48,384]{4,3,2,1,0:T(8,128)(2,1)S(1)}, u32[]{:S(2)}, u32[]{:S(2)}) collective-permute-start(bf16[4,2,3,48,384]{4,3,2,1,0:T(8,128)(2,1)} %get-tuple-element.12), channel_id=1, source_target_pairs={{0,2},{1,3},{2,4},{3,5},{4,6},{5,7},{6,8},{7,9},{8,10},{9,11},{10,... | collective-permute-start | bytes 2654216 | tf_op jit(solution)/shard_map/ppermute | solution.py:234
  57.8 5.8 %collective-permute-start.3 = (bf16[4,2,3,48,384]{4,3,2,1,0:T(8,128)(2,1)}, bf16[4,2,3,48,384]{4,3,2,1,0:T(8,128)(2,1)}, u32[]{:S(2)}, u32[]{:S(2)}) collective-permute-start(bf16[4,2,3,48,384]{4,3,2,1,0:T(8,128)(2,1)} %get-tuple-element.11), channel_id=1, source_target_pairs={{2,0},{3,1},{4,2},{5,3},{6,4},{7,5},{8,6},{9,7},{10,8},{11,9},{12,... | collective-permute-start | bytes 2654216 | tf_op jit(solution)/shard_map/ppermute | solution.py:235
  63.5 1.9 %collective-permute-start.5 = (bf16[8,2,3,48,384]{4,3,2,1,0:T(8,128)(2,1)S(1)}, bf16[8,2,3,48,384]{4,3,2,1,0:T(8,128)(2,1)}, u32[]{:S(2)}, u32[]{:S(2)}) collective-permute-start(bf16[8,2,3,48,384]{4,3,2,1,0:T(8,128)(2,1)S(1)} %all_to_all.15.refs_0_), channel_id=1, source_target_pairs={{0,64},{1,65},{2,66},{3,67},{4,68},{5,69},{6,70},{7,71},{8,72},{9,... | collective-permute-start | bytes 5308424 | tf_op jit(solution)/shard_map/ppermute | solution.py:236
  65.5 2.6 %shard_map.73 = bf16[8,1,3,48,384]{4,3,2,1,0:T(8,128)(2,1)} custom-call(bf16[3,48,3072]{2,1,0:T(8,128)(2,1)} %refs_0_.2, f32[1,128]{1,0:T(1,128)} %bitcast.8), custom_call_target="tpu_custom_call" | custom-call | tf_op jit(solution)/shard_map/pallas_call | solution.py:75
  68.1 3.6 %all-to-all-start = ((bf16[8,1,3,48,384]{4,3,2,1,0:T(8,128)(2,1)}), bf16[8,1,3,48,384]{4,3,2,1,0:T(8,128)(2,1)S(1)}, u32[]{:S(2)}, u32[]{:S(2)}) async-start(bf16[8,1,3,48,384]{4,3,2,1,0:T(8,128)(2,1)} %shard_map.73), calls=%async_computation | async-start | bytes 1769472 | tf_op jit(solution)/shard_map/all_to_all | solution.py:233
  71.7 0.1 copy.10
  71.8 0.7 pad_add_fusion
  72.4 4.0 %collective-permute-start = (s32[3,10]{1,0:T(4,128)}, s32[3,10]{1,0:T(4,128)S(1)}, u32[]{:S(2)}, u32[]{:S(2)}) collective-permute-start(s32[3,10]{1,0:T(4,128)} %pad_add_fusion), channel_id=1, source_target_pairs={{0,1},{1,0},{2,3},{3,2},{4,5},{5,4},{6,7},{7,6},{8,9},{9,8},{10,11... | collective-permute-start | bytes 368 | tf_op jit(solution)/shard_map/ppermute | solution.py:220
  76.5 1.4 collective-permute-done.1.refs_0_
  78.0 1.9 %collective-permute-start.2 = (bf16[4,2,3,48,384]{4,3,2,1,0:T(8,128)(2,1)S(1)}, bf16[4,2,3,48,384]{4,3,2,1,0:T(8,128)(2,1)}, u32[]{:S(2)}, u32[]{:S(2)}) collective-permute-start(bf16[4,2,3,48,384]{4,3,2,1,0:T(8,128)(2,1)S(1)} %collective-permute-done.1.refs_0_), channel_id=1, source_target_pairs={{0,64},{1,65},{2,66},{3,67},{4,68},{5,69},{6,70},{7,71},{8,72},{9,... | collective-permute-start | bytes 2654216 | tf_op jit(solution)/shard_map/ppermute | solution.py:237
  79.9 2.4 %collective-permute-start.4 = (bf16[4,2,3,48,384]{4,3,2,1,0:T(8,128)(2,1)}, bf16[4,2,3,48,384]{4,3,2,1,0:T(8,128)(2,1)}, u32[]{:S(2)}, u32[]{:S(2)}) collective-permute-start(bf16[4,2,3,48,384]{4,3,2,1,0:T(8,128)(2,1)} %collective-permute-done.3.refs_2_), channel_id=1, source_target_pairs={{0,64},{1,65},{2,66},{3,67},{4,68},{5,69},{6,70},{7,71},{8,72},{9,... | collective-permute-start | bytes 2654216 | tf_op jit(solution)/shard_map/ppermute | solution.py:238
  82.3 11.9 %collective-permute-done = s32[3,10]{1,0:T(4,128)S(1)} collective-permute-done((s32[3,10]{1,0:T(4,128)}, s32[3,10]{1,0:T(4,128)S(1)}, u32[]{:S(2)}, u32[]{:S(2)}) %collective-permute-start) | collective-permute-done | bytes 152 | tf_op jit(solution)/shard_map/ppermute | solution.py:220
  94.3 0.2 slice_reduce_fusion
  94.5 0.1 iota_compare_fusion.1
  94.6 0.3 fusion.1
  94.9 0.1 copy.11
  95.0 0.1 all-to-all-done.query
  95.1 12.4 %shard_map.75 = (f32[6,3,192,128]{3,2,1,0:T(8,128)S(1)}, f32[6,3,192,128]{3,2,1,0:T(8,128)S(1)}, f32[6,3,192,128]{3,2,1,0:T(8,128)S(1)}) custom-call(s32[6,9]{1,0:T(8,128)S(1)} %convert_element_type.3.live_ref, bf16[8,1,3,48,384]{4,3,2,1,0:T(8,128)(2,1)S(1)} %all-to-all-done.query, bf16[8,2,3,48,384]{4,3,2,1,0:T(8,128)(2,1)S(1)} %all_to_all.15.refs_0_, ...), custom_call_target="tpu_custom_call" | custom-call | tf_op jit(solution)/shard_map/pallas_call | solution.py:183
  107.5 8.9 %shard_map.76 = bf16[8,3,48,384]{3,2,1,0:T(8,128)(2,1)S(1)} custom-call(s32[6,9]{1,0:T(8,128)S(1)} %convert_element_type.3.live_ref, bf16[8,1,3,48,384]{4,3,2,1,0:T(8,128)(2,1)S(1)} %all-to-all-done.query, bf16[4,2,3,48,384]{4,3,2,1,0:T(8,128)(2,1)S(1)} %collective-permute-done.1.refs_0_, bf16[4,2,3,48,384]{4,3,2,1,0:T(8,128)(2,1)} %collective-permute-done.2.refs_1_, ...), custom_call_target="tpu_custom_call" | custom-call | tf_op jit(solution)/shard_map/pallas_call | solution.py:183
  116.4 29.3 %all_to_all.16.ref = bf16[8,3,48,384]{3,2,1,0:T(8,128)(2,1)} all-to-all(bf16[8,3,48,384]{3,2,1,0:T(8,128)(2,1)S(1)} %shard_map.76), channel_id=1, replica_groups=mesh['yhi'=4,'core'=2,'z'=8,'x'=4,'ylo'=2] {'ylo','yhi'}, dimensions={0} | all-to-all | bytes 1769472 | tf_op jit(solution)/shard_map/all_to_all | solution.py:242
  145.7 2.2 %unpack.1 = bf16[3,48,3072]{2,1,0:T(8,128)(2,1)} custom-call(bf16[8,3,48,384]{3,2,1,0:T(8,128)(2,1)} %all_to_all.16.ref), custom_call_target="tpu_custom_call" | custom-call | tf_op jit(solution)/shard_map/unpack/pallas_call | solution.py:207
  (14 shorter events, 0.2 us)
Async XLA Ops:
  54.4 23.6 %collective-permute-start.1 = (bf16[4,2,3,48,384]{4,3,2,1,0:T(8,128)(2,1)}, bf16[4,2,3,48,384]{4,3,2,1,0:T(8,128)(2,1)S(1)}, u32[]{:S(2)}, u32[]{:S(2)}) collective-permute-start(bf16[4,2,3,48,384]{4,3,2,1,0:T(8,128)(2,1)} %get-tuple-element.12), channel_id=1, source_target_pairs={{0,2},{1,3},{2,4},{3,5},{4,6},{5,7},{6,8},{7,9},{8,10},{9,11},{10,... | collective-permute-start | bytes 2654216 | tf_op jit(solution)/shard_map/ppermute | solution.py:234
  57.8 22.1 %collective-permute-start.3 = (bf16[4,2,3,48,384]{4,3,2,1,0:T(8,128)(2,1)}, bf16[4,2,3,48,384]{4,3,2,1,0:T(8,128)(2,1)}, u32[]{:S(2)}, u32[]{:S(2)}) collective-permute-start(bf16[4,2,3,48,384]{4,3,2,1,0:T(8,128)(2,1)} %get-tuple-element.11), channel_id=1, source_target_pairs={{2,0},{3,1},{4,2},{5,3},{6,4},{7,5},{8,6},{9,7},{10,8},{11,9},{12,... | collective-permute-start | bytes 2654216 | tf_op jit(solution)/shard_map/ppermute | solution.py:235
  63.5 31.6 %collective-permute-start.5 = (bf16[8,2,3,48,384]{4,3,2,1,0:T(8,128)(2,1)S(1)}, bf16[8,2,3,48,384]{4,3,2,1,0:T(8,128)(2,1)}, u32[]{:S(2)}, u32[]{:S(2)}) collective-permute-start(bf16[8,2,3,48,384]{4,3,2,1,0:T(8,128)(2,1)S(1)} %all_to_all.15.refs_0_), channel_id=1, source_target_pairs={{0,64},{1,65},{2,66},{3,67},{4,68},{5,69},{6,70},{7,71},{8,72},{9,... | collective-permute-start | bytes 5308424 | tf_op jit(solution)/shard_map/ppermute | solution.py:236
  65.5 6.2 %copy-start.1 = (s32[3]{0:T(128)S(1)}, s32[3]{0:T(128)}, u32[]{:S(2)}) copy-start(s32[3]{0:T(128)} %param.13) | copy-start | bytes 40
  65.5 6.3 %copy-start = (s32[3,9]{1,0:T(4,128)S(1)}, s32[3,9]{1,0:T(4,128)}, u32[]{:S(2)}) copy-start(s32[3,9]{1,0:T(4,128)} %param.12) | copy-start | bytes 328
  68.1 27.0 %all-to-all-start = ((bf16[8,1,3,48,384]{4,3,2,1,0:T(8,128)(2,1)}), bf16[8,1,3,48,384]{4,3,2,1,0:T(8,128)(2,1)S(1)}, u32[]{:S(2)}, u32[]{:S(2)}) async-start(bf16[8,1,3,48,384]{4,3,2,1,0:T(8,128)(2,1)} %shard_map.73), calls=%async_computation | async-start | bytes 1769472 | tf_op jit(solution)/shard_map/all_to_all | solution.py:233
  72.4 21.8 %collective-permute-start = (s32[3,10]{1,0:T(4,128)}, s32[3,10]{1,0:T(4,128)S(1)}, u32[]{:S(2)}, u32[]{:S(2)}) collective-permute-start(s32[3,10]{1,0:T(4,128)} %pad_add_fusion), channel_id=1, source_target_pairs={{0,1},{1,0},{2,3},{3,2},{4,5},{5,4},{6,7},{7,6},{8,9},{9,8},{10,11... | collective-permute-start | bytes 368 | tf_op jit(solution)/shard_map/ppermute | solution.py:220
  78.0 29.5 %collective-permute-start.2 = (bf16[4,2,3,48,384]{4,3,2,1,0:T(8,128)(2,1)S(1)}, bf16[4,2,3,48,384]{4,3,2,1,0:T(8,128)(2,1)}, u32[]{:S(2)}, u32[]{:S(2)}) collective-permute-start(bf16[4,2,3,48,384]{4,3,2,1,0:T(8,128)(2,1)S(1)} %collective-permute-done.1.refs_0_), channel_id=1, source_target_pairs={{0,64},{1,65},{2,66},{3,67},{4,68},{5,69},{6,70},{7,71},{8,72},{9,... | collective-permute-start | bytes 2654216 | tf_op jit(solution)/shard_map/ppermute | solution.py:237
  79.9 27.6 %collective-permute-start.4 = (bf16[4,2,3,48,384]{4,3,2,1,0:T(8,128)(2,1)}, bf16[4,2,3,48,384]{4,3,2,1,0:T(8,128)(2,1)}, u32[]{:S(2)}, u32[]{:S(2)}) collective-permute-start(bf16[4,2,3,48,384]{4,3,2,1,0:T(8,128)(2,1)} %collective-permute-done.3.refs_2_), channel_id=1, source_target_pairs={{0,64},{1,65},{2,66},{3,67},{4,68},{5,69},{6,70},{7,71},{8,72},{9,... | collective-permute-start | bytes 2654216 | tf_op jit(solution)/shard_map/ppermute | solution.py:238

commit v3 on v2

--- a/solution.py
+++ b/solution.py
@@ -20,6 +20,7 @@
 AXES = ("yhi", "core", "z", "x", "ylo")
 RING = ("ylo", "yhi")
 HEADS = 3
+AT_ONCE = 4
 ROWS = 4 * LOC
 KEYS = 8 * LOC
 SLABS = {"first": 2, "last": 1}
@@ -55,7 +56,7 @@
     for which, has_gain in enumerate(normed):
         ref = refs.pop(0)
         gain = refs.pop(0) if has_gain else None
-        for chip in range(8):
+        for chip in range(AT_ONCE):
             for head in range(HEADS):
                 at = (chip * HEADS + head) * HD
                 part = ref[:, :, at : at + HD]
@@ -67,15 +68,19 @@
 
 
 def pack(*pairs):
-    whole = pl.BlockSpec(memory_space=pltpu.VMEM)
-    operands = []
+    width = AT_ONCE * HEADS * HD
+    operands, specs = [], []
     for array, gain in pairs:
         operands += [array] if gain is None else [array, gain.reshape(1, HD)]
+        specs.append(pl.BlockSpec((TD, LOC, width), lambda i: (0, 0, i)))
+        if gain is not None:
+            specs.append(pl.BlockSpec((1, HD), lambda i: (0, 0)))
     shape = (8, len(pairs), TD, LOC, HEADS * HD)
     return pl.pallas_call(
         functools.partial(pack_kernel, [gain is not None for _, gain in pairs]),
-        in_specs=[whole] * len(operands),
-        out_specs=whole,
+        grid=(8 // AT_ONCE,),
+        in_specs=specs,
+        out_specs=pl.BlockSpec((AT_ONCE,) + shape[1:], lambda i: (i, 0, 0, 0, 0)),
         out_shape=jax.ShapeDtypeStruct(shape, jnp.bfloat16),
     )(*operands)
 
@@ -198,16 +203,17 @@
 
 def unpack_kernel(ref, out_ref):
     width = ref.shape[-1]
-    for chip in range(8):
+    for chip in range(ref.shape[0]):
         out_ref[:, :, chip * width : (chip + 1) * width] = ref[chip]
 
 
 def unpack(block):
-    whole = pl.BlockSpec(memory_space=pltpu.VMEM)
+    width = block.shape[-1]
     return pl.pallas_call(
         unpack_kernel,
-        in_specs=[whole],
-        out_specs=whole,
+        grid=(8 // AT_ONCE,),
+        in_specs=[pl.BlockSpec((AT_ONCE, TD, LOC, width), lambda i: (i, 0, 0, 0))],
+        out_specs=pl.BlockSpec((TD, LOC, AT_ONCE * width), lambda i: (0, 0, i)),
         out_shape=jax.ShapeDtypeStruct((TD, LOC, 24 * HD), jnp.bfloat16),
         name="unpack",
     )(block)

time: 148 us -> 148 us (level)
  no operation moved by 1% of the time
where the time goes in v3:
time: 148 us; the launch traced here: 147 us
  blocking collectives  79 us (53%)
  Pallas kernels  28.5 us (19%)
  starting transfers between devices  22.9 us (15%)
  waiting for transfers between devices  13.5 us (9%)
  local copies, waits for them, and re-layouts  1.8 us (1%)
    all_to_all x1, blocking collectives, compute(): own = lax.all_to_all(block, RING, 0, 0, tiled=True)  49.7 us
    all_to_all x1, blocking collectives, compute(): done = lax.all_to_all(done, RING, 0, 0, tiled=True)  29.3 us
    pallas_call x2, Pallas kernels, attend(): pl.pallas_call(functools.partial(attend_kernel, part, nh), in_specs=[pl.B...  21.3 us
    ppermute x1, waiting for transfers between devices, compute(): other = lax.ppermute(table, AXES, SWAP_SLAB)  11.8 us
    ppermute x1, starting transfers between devices, compute(): next_own = lax.ppermute(own[:4], AXES, BACKWARD)  5.76 us
    pallas_call x2, Pallas kernels, pack(): pl.pallas_call(functools.partial(pack_kernel, [gain is not None for _, ga...  5.22 us
    ppermute x1, starting transfers between devices, compute(): other = lax.ppermute(table, AXES, SWAP_SLAB)  3.97 us
    all_to_all x1, starting transfers between devices, compute(): query = lax.all_to_all(block, RING, 0, 0, tiled=True)  3.55 us
  transfers between devices with their start and end apart: 7, of which 3 were waited for; matrix products, arithmetic and copies ran while one was open for 1% of the time, Pallas kernels for 10%

profile of v3, /device:TPU:256, one launch (start us, length us, event | category | flops | bytes accessed | tf_op | source)
XLA Modules:
  0.0 147.0 jit_solution(7488243767764108851)
XLA Ops:
  0.0 2.8 %shard_map.74 = bf16[8,2,3,48,384]{4,3,2,1,0:T(8,128)(2,1)} custom-call(bf16[3,48,3072]{2,1,0:T(8,128)(2,1)} %refs_0_.3, f32[1,128]{1,0:T(1,128)} %bitcast.9, bf16[3,48,3072]{2,1,0:T(8,128)(2,1)} %refs_2_.1), custom_call_target="tpu_custom_call" | custom-call | tf_op jit(solution)/shard_map/pallas_call | solution.py:79
  2.8 49.7 %all_to_all.15.refs_0_ = bf16[8,2,3,48,384]{4,3,2,1,0:T(8,128)(2,1)S(1)} all-to-all(bf16[8,2,3,48,384]{4,3,2,1,0:T(8,128)(2,1)} %shard_map.74), channel_id=1, replica_groups=mesh['yhi'=4,'core'=2,'z'=8,'x'=4,'ylo'=2] {'ylo','yhi'}, dimensions={0} | all-to-all | bytes 3538944 | tf_op jit(solution)/shard_map/all_to_all | solution.py:237
  52.5 1.4 fusion.4
  53.9 3.4 %collective-permute-start.1 = (bf16[4,2,3,48,384]{4,3,2,1,0:T(8,128)(2,1)}, bf16[4,2,3,48,384]{4,3,2,1,0:T(8,128)(2,1)S(1)}, u32[]{:S(2)}, u32[]{:S(2)}) collective-permute-start(bf16[4,2,3,48,384]{4,3,2,1,0:T(8,128)(2,1)} %get-tuple-element.12), channel_id=1, source_target_pairs={{0,2},{1,3},{2,4},{3,5},{4,6},{5,7},{6,8},{7,9},{8,10},{9,11},{10,... | collective-permute-start | bytes 2654216 | tf_op jit(solution)/shard_map/ppermute | solution.py:240
  57.3 5.8 %collective-permute-start.3 = (bf16[4,2,3,48,384]{4,3,2,1,0:T(8,128)(2,1)}, bf16[4,2,3,48,384]{4,3,2,1,0:T(8,128)(2,1)}, u32[]{:S(2)}, u32[]{:S(2)}) collective-permute-start(bf16[4,2,3,48,384]{4,3,2,1,0:T(8,128)(2,1)} %get-tuple-element.11), channel_id=1, source_target_pairs={{2,0},{3,1},{4,2},{5,3},{6,4},{7,5},{8,6},{9,7},{10,8},{11,9},{12,... | collective-permute-start | bytes 2654216 | tf_op jit(solution)/shard_map/ppermute | solution.py:241
  63.0 1.9 %collective-permute-start.5 = (bf16[8,2,3,48,384]{4,3,2,1,0:T(8,128)(2,1)S(1)}, bf16[8,2,3,48,384]{4,3,2,1,0:T(8,128)(2,1)}, u32[]{:S(2)}, u32[]{:S(2)}) collective-permute-start(bf16[8,2,3,48,384]{4,3,2,1,0:T(8,128)(2,1)S(1)} %all_to_all.15.refs_0_), channel_id=1, source_target_pairs={{0,64},{1,65},{2,66},{3,67},{4,68},{5,69},{6,70},{7,71},{8,72},{9,... | collective-permute-start | bytes 5308424 | tf_op jit(solution)/shard_map/ppermute | solution.py:242
  65.0 2.4 %shard_map.73 = bf16[8,1,3,48,384]{4,3,2,1,0:T(8,128)(2,1)} custom-call(bf16[3,48,3072]{2,1,0:T(8,128)(2,1)} %refs_0_.2, f32[1,128]{1,0:T(1,128)} %bitcast.8), custom_call_target="tpu_custom_call" | custom-call | tf_op jit(solution)/shard_map/pallas_call | solution.py:79
  67.4 3.6 %all-to-all-start = ((bf16[8,1,3,48,384]{4,3,2,1,0:T(8,128)(2,1)}), bf16[8,1,3,48,384]{4,3,2,1,0:T(8,128)(2,1)S(1)}, u32[]{:S(2)}, u32[]{:S(2)}) async-start(bf16[8,1,3,48,384]{4,3,2,1,0:T(8,128)(2,1)} %shard_map.73), calls=%async_computation | async-start | bytes 1769472 | tf_op jit(solution)/shard_map/all_to_all | solution.py:239
  71.0 0.1 copy.10
  71.1 0.7 pad_add_fusion
  71.8 4.0 %collective-permute-start = (s32[3,10]{1,0:T(4,128)}, s32[3,10]{1,0:T(4,128)S(1)}, u32[]{:S(2)}, u32[]{:S(2)}) collective-permute-start(s32[3,10]{1,0:T(4,128)} %pad_add_fusion), channel_id=1, source_target_pairs={{0,1},{1,0},{2,3},{3,2},{4,5},{5,4},{6,7},{7,6},{8,9},{9,8},{10,11... | collective-permute-start | bytes 368 | tf_op jit(solution)/shard_map/ppermute | solution.py:226
  75.8 1.6 %collective-permute-done.1.refs_0_ = bf16[4,2,3,48,384]{4,3,2,1,0:T(8,128)(2,1)S(1)} collective-permute-done((bf16[4,2,3,48,384]{4,3,2,1,0:T(8,128)(2,1)}, bf16[4,2,3,48,384]{4,3,2,1,0:T(8,128)(2,1)S(1)}, u32[]{:S(2)}, u32[]{:S(2)}) %collective-permute-start.1) | collective-permute-done | bytes 884768 | tf_op jit(solution)/shard_map/ppermute | solution.py:240
  77.5 1.9 %collective-permute-start.2 = (bf16[4,2,3,48,384]{4,3,2,1,0:T(8,128)(2,1)S(1)}, bf16[4,2,3,48,384]{4,3,2,1,0:T(8,128)(2,1)}, u32[]{:S(2)}, u32[]{:S(2)}) collective-permute-start(bf16[4,2,3,48,384]{4,3,2,1,0:T(8,128)(2,1)S(1)} %collective-permute-done.1.refs_0_), channel_id=1, source_target_pairs={{0,64},{1,65},{2,66},{3,67},{4,68},{5,69},{6,70},{7,71},{8,72},{9,... | collective-permute-start | bytes 2654216 | tf_op jit(solution)/shard_map/ppermute | solution.py:243
  79.4 2.4 %collective-permute-start.4 = (bf16[4,2,3,48,384]{4,3,2,1,0:T(8,128)(2,1)}, bf16[4,2,3,48,384]{4,3,2,1,0:T(8,128)(2,1)}, u32[]{:S(2)}, u32[]{:S(2)}) collective-permute-start(bf16[4,2,3,48,384]{4,3,2,1,0:T(8,128)(2,1)} %collective-permute-done.3.refs_2_), channel_id=1, source_target_pairs={{0,64},{1,65},{2,66},{3,67},{4,68},{5,69},{6,70},{7,71},{8,72},{9,... | collective-permute-start | bytes 2654216 | tf_op jit(solution)/shard_map/ppermute | solution.py:244
  81.8 11.8 %collective-permute-done = s32[3,10]{1,0:T(4,128)S(1)} collective-permute-done((s32[3,10]{1,0:T(4,128)}, s32[3,10]{1,0:T(4,128)S(1)}, u32[]{:S(2)}, u32[]{:S(2)}) %collective-permute-start) | collective-permute-done | bytes 152 | tf_op jit(solution)/shard_map/ppermute | solution.py:226
  93.6 0.2 slice_reduce_fusion
  93.8 0.1 iota_compare_fusion.1
  93.9 0.3 fusion.1
  94.2 0.1 copy.11
  94.3 0.1 all-to-all-done.query
  94.4 12.4 %shard_map.75 = (f32[6,3,192,128]{3,2,1,0:T(8,128)S(1)}, f32[6,3,192,128]{3,2,1,0:T(8,128)S(1)}, f32[6,3,192,128]{3,2,1,0:T(8,128)S(1)}) custom-call(s32[6,9]{1,0:T(8,128)S(1)} %convert_element_type.3.live_ref, bf16[8,1,3,48,384]{4,3,2,1,0:T(8,128)(2,1)S(1)} %all-to-all-done.query, bf16[8,2,3,48,384]{4,3,2,1,0:T(8,128)(2,1)S(1)} %all_to_all.15.refs_0_, ...), custom_call_target="tpu_custom_call" | custom-call | tf_op jit(solution)/shard_map/pallas_call | solution.py:188
  106.8 8.9 %shard_map.76 = bf16[8,3,48,384]{3,2,1,0:T(8,128)(2,1)S(1)} custom-call(s32[6,9]{1,0:T(8,128)S(1)} %convert_element_type.3.live_ref, bf16[8,1,3,48,384]{4,3,2,1,0:T(8,128)(2,1)S(1)} %all-to-all-done.query, bf16[4,2,3,48,384]{4,3,2,1,0:T(8,128)(2,1)S(1)} %collective-permute-done.1.refs_0_, bf16[4,2,3,48,384]{4,3,2,1,0:T(8,128)(2,1)} %collective-permute-done.2.refs_1_, ...), custom_call_target="tpu_custom_call" | custom-call | tf_op jit(solution)/shard_map/pallas_call | solution.py:188
  115.8 29.3 %all_to_all.16.ref = bf16[8,3,48,384]{3,2,1,0:T(8,128)(2,1)} all-to-all(bf16[8,3,48,384]{3,2,1,0:T(8,128)(2,1)S(1)} %shard_map.76), channel_id=1, replica_groups=mesh['yhi'=4,'core'=2,'z'=8,'x'=4,'ylo'=2] {'ylo','yhi'}, dimensions={0} | all-to-all | bytes 1769472 | tf_op jit(solution)/shard_map/all_to_all | solution.py:248
  145.0 2.0 %unpack.1 = bf16[3,48,3072]{2,1,0:T(8,128)(2,1)} custom-call(bf16[8,3,48,384]{3,2,1,0:T(8,128)(2,1)} %all_to_all.16.ref), custom_call_target="tpu_custom_call" | custom-call | tf_op jit(solution)/shard_map/unpack/pallas_call | solution.py:212
  (14 shorter events, 0.2 us)
Async XLA Ops:
  53.9 23.6 %collective-permute-start.1 = (bf16[4,2,3,48,384]{4,3,2,1,0:T(8,128)(2,1)}, bf16[4,2,3,48,384]{4,3,2,1,0:T(8,128)(2,1)S(1)}, u32[]{:S(2)}, u32[]{:S(2)}) collective-permute-start(bf16[4,2,3,48,384]{4,3,2,1,0:T(8,128)(2,1)} %get-tuple-element.12), channel_id=1, source_target_pairs={{0,2},{1,3},{2,4},{3,5},{4,6},{5,7},{6,8},{7,9},{8,10},{9,11},{10,... | collective-permute-start | bytes 2654216 | tf_op jit(solution)/shard_map/ppermute | solution.py:240
  57.3 22.1 %collective-permute-start.3 = (bf16[4,2,3,48,384]{4,3,2,1,0:T(8,128)(2,1)}, bf16[4,2,3,48,384]{4,3,2,1,0:T(8,128)(2,1)}, u32[]{:S(2)}, u32[]{:S(2)}) collective-permute-start(bf16[4,2,3,48,384]{4,3,2,1,0:T(8,128)(2,1)} %get-tuple-element.11), channel_id=1, source_target_pairs={{2,0},{3,1},{4,2},{5,3},{6,4},{7,5},{8,6},{9,7},{10,8},{11,9},{12,... | collective-permute-start | bytes 2654216 | tf_op jit(solution)/shard_map/ppermute | solution.py:241
  63.0 31.4 %collective-permute-start.5 = (bf16[8,2,3,48,384]{4,3,2,1,0:T(8,128)(2,1)S(1)}, bf16[8,2,3,48,384]{4,3,2,1,0:T(8,128)(2,1)}, u32[]{:S(2)}, u32[]{:S(2)}) collective-permute-start(bf16[8,2,3,48,384]{4,3,2,1,0:T(8,128)(2,1)S(1)} %all_to_all.15.refs_0_), channel_id=1, source_target_pairs={{0,64},{1,65},{2,66},{3,67},{4,68},{5,69},{6,70},{7,71},{8,72},{9,... | collective-permute-start | bytes 5308424 | tf_op jit(solution)/shard_map/ppermute | solution.py:242
  65.0 6.0 %copy-start.1 = (s32[3]{0:T(128)S(1)}, s32[3]{0:T(128)}, u32[]{:S(2)}) copy-start(s32[3]{0:T(128)} %param.13) | copy-start | bytes 40
  65.0 6.1 %copy-start = (s32[3,9]{1,0:T(4,128)S(1)}, s32[3,9]{1,0:T(4,128)}, u32[]{:S(2)}) copy-start(s32[3,9]{1,0:T(4,128)} %param.12) | copy-start | bytes 328
  67.4 27.0 %all-to-all-start = ((bf16[8,1,3,48,384]{4,3,2,1,0:T(8,128)(2,1)}), bf16[8,1,3,48,384]{4,3,2,1,0:T(8,128)(2,1)S(1)}, u32[]{:S(2)}, u32[]{:S(2)}) async-start(bf16[8,1,3,48,384]{4,3,2,1,0:T(8,128)(2,1)} %shard_map.73), calls=%async_computation | async-start | bytes 1769472 | tf_op jit(solution)/shard_map/all_to_all | solution.py:239
  71.8 21.8 %collective-permute-start = (s32[3,10]{1,0:T(4,128)}, s32[3,10]{1,0:T(4,128)S(1)}, u32[]{:S(2)}, u32[]{:S(2)}) collective-permute-start(s32[3,10]{1,0:T(4,128)} %pad_add_fusion), channel_id=1, source_target_pairs={{0,1},{1,0},{2,3},{3,2},{4,5},{5,4},{6,7},{7,6},{8,9},{9,8},{10,11... | collective-permute-start | bytes 368 | tf_op jit(solution)/shard_map/ppermute | solution.py:226
  77.5 29.3 %collective-permute-start.2 = (bf16[4,2,3,48,384]{4,3,2,1,0:T(8,128)(2,1)S(1)}, bf16[4,2,3,48,384]{4,3,2,1,0:T(8,128)(2,1)}, u32[]{:S(2)}, u32[]{:S(2)}) collective-permute-start(bf16[4,2,3,48,384]{4,3,2,1,0:T(8,128)(2,1)S(1)} %collective-permute-done.1.refs_0_), channel_id=1, source_target_pairs={{0,64},{1,65},{2,66},{3,67},{4,68},{5,69},{6,70},{7,71},{8,72},{9,... | collective-permute-start | bytes 2654216 | tf_op jit(solution)/shard_map/ppermute | solution.py:243
  79.4 27.4 %collective-permute-start.4 = (bf16[4,2,3,48,384]{4,3,2,1,0:T(8,128)(2,1)}, bf16[4,2,3,48,384]{4,3,2,1,0:T(8,128)(2,1)}, u32[]{:S(2)}, u32[]{:S(2)}) collective-permute-start(bf16[4,2,3,48,384]{4,3,2,1,0:T(8,128)(2,1)} %collective-permute-done.3.refs_2_), channel_id=1, source_target_pairs={{0,64},{1,65},{2,66},{3,67},{4,68},{5,69},{6,70},{7,71},{8,72},{9,... | collective-permute-start | bytes 2654216 | tf_op jit(solution)/shard_map/ppermute | solution.py:244
